TPU v7x, 32 devices: a whole 2x2x4 slice. The times are simulated.
32 devices in a mesh: seq: 16 (over z, y, core), blk: 2 (over x).
Axes of the slice: x: 2, y: 2, z: 4, core: 2. Of those that a mesh axis runs over, the one named last changes fastest.
Arguments:
- tokens: bfloat16 [32, 1024, 512], P('seq', 'blk'), may hold values from -6 to 6
- memory: bfloat16 [32, 512, 512], P('seq', 'blk'), may hold values from -6 to 6
- segment_ends: int32 [32, 1024], P('seq', 'blk'), may hold values from 1 to 8192, as said below
- memory_ends: int32 [32, 512], P('seq', 'blk'), may hold values from -4088 to 0, as said below
- segment_counts: int32 [32], P('seq'), may hold values from 512 to 1024, as said below
- memory_lengths: int32 [32], P('seq'), may hold values from 128 to 512, as said below
- first_gain: float32 [512], replicated, may hold values from 0.5 to 1.5
- first_shift: float32 [512], replicated, may hold values from -1.2 to 1.2
- query_weight: bfloat16 [512, 512], replicated, may hold values from -0.25 to 0.25
- key_weight: bfloat16 [512, 512], replicated, may hold values from -0.25 to 0.25
- value_weight: bfloat16 [512, 512], replicated, may hold values from -0.25 to 0.25
- out_weight: bfloat16 [512, 512], replicated, may hold values from -2 to 2
- head_slopes: float32 [8], replicated, may hold values from 1e-05 to 0.03
- second_gain: float32 [512], replicated, may hold values from 0.5 to 1.5
- second_shift: float32 [512], replicated, may hold values from -1.2 to 1.2
- hidden_weight: bfloat16 [512, 2048], replicated, may hold values from -0.25 to 0.25
- output_weight: bfloat16 [2048, 512], replicated, may hold values from -0.125 to 0.125
- output_grad: bfloat16 [32, 1024, 512], P('seq', 'blk'), may hold values from -6 to 6
Outputs:
- layer_out: bfloat16 [32, 1024, 512], P('seq', 'blk')
- input_grad: bfloat16 [32, 1024, 512], P('seq', 'blk')
- grad_first_gain: float32 [512], replicated
- grad_first_shift: float32 [512], replicated
- grad_query_weight: float32 [512, 512], replicated
- grad_key_weight: float32 [512, 512], replicated
- grad_value_weight: float32 [512, 512], replicated
- grad_out_weight: float32 [512, 512], replicated
- grad_head_slopes: float32 [8], replicated
- grad_second_gain: float32 [512], replicated
- grad_second_shift: float32 [512], replicated
- grad_hidden_weight: float32 [512, 2048], replicated
- grad_output_weight: float32 [2048, 512], replicated
Inputs may be any that keep to these rules, and one draw needn't show every extreme that they name: `segment_ends`: each row rises strictly by 1 to 8 bytes from slot to slot; the first slot ends 1 to 8 bytes after the row's last memory end. In some sequence every step is 8 bytes; in another the first slot ends 1 byte after its memory. `memory_ends`: each row rises strictly by 1 to 8 bytes from entry to entry and its last entry is 0; in some sequence every step is 8 bytes. `segment_counts`: slots 0 to count - 1 of a sequence hold segments, the others are empty; some sequence uses all 1024 slots and some exactly half of them. `memory_lengths`: the last length memory rows of a sequence are valid; some sequence has all 512 and some a quarter.
All inputs are finite; a program needn't handle non-finite values.
Results may differ from a plain program's by a relative error of at most 0.022.
Values may be sent and summed in bfloat16 or wider, within the bound.
A program may use at most 256 MiB of HBM per device.

v0:
```python
import math

import jax
import jax.numpy as jnp
from jax import lax
from jax.sharding import PartitionSpec as P

epsilon = 1e-05
far_order = 1073741824


def layer_norm(values, gain, shift):
    centred = values - jnp.mean(values, axis=-1, keepdims=True)
    spread = jnp.mean(centred * centred, axis=-1, keepdims=True)
    return centred * lax.rsqrt(spread + epsilon) * gain + shift


def block_scores(
    q_heads, key_block, q_ends, key_order, key_ends, q_index, head_slopes, score_scale
):
    scores = (
        jnp.einsum("qhd,khd->hqk", q_heads, key_block, preferred_element_type=jnp.float32)
        * score_scale
    )
    distance = (q_ends[:, None] - key_ends[None, :]).astype(jnp.float32)
    scores = scores - head_slopes[:, None, None] * distance[None]
    allowed = key_order[None, :] <= q_index[:, None]
    return (jnp.where(allowed[None], scores, -1e30), distance)


def per_device(
    tokens,
    memory,
    segment_ends,
    memory_ends,
    segment_counts,
    memory_lengths,
    first_gain,
    first_shift,
    query_weight,
    key_weight,
    value_weight,
    out_weight,
    head_slopes,
    second_gain,
    second_shift,
    hidden_weight,
    output_weight,
    output_grad,
):
    seq_count, slot_count, model_width = tokens.shape
    mem_count = memory.shape[1]
    head_count = head_slopes.shape[0]
    head_dim = model_width // head_count
    score_scale = 1.0 / math.sqrt(head_dim)
    key_rows = mem_count + slot_count
    blocks = lax.axis_size("blk")
    my_block = lax.axis_index("blk")
    x_float = tokens.astype(jnp.float32)
    mem_float = memory.astype(jnp.float32)
    normed = layer_norm(x_float, first_gain, first_shift).astype(jnp.bfloat16)
    mem_normed = layer_norm(mem_float, first_gain, first_shift).astype(jnp.bfloat16)
    key_input = jnp.concatenate([mem_normed, normed], axis=1)
    query = jnp.einsum(
        "std,de->ste", normed, query_weight, preferred_element_type=jnp.float32
    ).astype(jnp.bfloat16)
    pair_weight = jnp.concatenate([key_weight, value_weight], axis=1)
    key_value = jnp.einsum(
        "srd,de->rse", key_input, pair_weight, preferred_element_type=jnp.float32
    ).astype(jnp.bfloat16)
    mem_index = my_block * mem_count + jnp.arange(mem_count, dtype=jnp.int32)
    slot_index = my_block * slot_count + jnp.arange(slot_count, dtype=jnp.int32)
    mem_order = jnp.where(
        mem_index[None, :] >= mem_count * blocks - memory_lengths[:, None], -1, far_order
    )
    slot_order = jnp.where(
        slot_index[None, :] < segment_counts[:, None], slot_index[None, :], far_order
    )
    key_meta = jnp.stack(
        [
            jnp.concatenate([mem_order, slot_order], axis=1),
            jnp.concatenate([memory_ends, segment_ends], axis=1),
        ]
    )
    all_pairs, all_meta = (
        lax.all_gather(key_value, "blk", axis=0, tiled=True),
        lax.all_gather(key_meta, "blk", axis=2, tiled=True),
    )
    query_heads = query.reshape(seq_count, slot_count, head_count, head_dim)

    def pick(seq_index):
        pair_rows = lax.dynamic_index_in_dim(all_pairs, seq_index, 1, keepdims=False)
        meta_rows = lax.dynamic_index_in_dim(all_meta, seq_index, 1, keepdims=False)
        key_heads = pair_rows[:, :model_width].reshape(-1, key_rows, head_count, head_dim)
        value_heads = pair_rows[:, model_width:].reshape(-1, key_rows, head_count, head_dim)
        return (
            key_heads,
            value_heads,
            meta_rows[0].reshape(-1, key_rows),
            meta_rows[1].reshape(-1, key_rows),
        )

    def attend(seq_index):
        key_heads, value_heads, key_order, key_ends = pick(seq_index)
        q_heads = lax.dynamic_index_in_dim(query_heads, seq_index, 0, keepdims=False)
        q_ends = lax.dynamic_index_in_dim(segment_ends, seq_index, 0, keepdims=False)

        def stats_step(running, pieces):
            scores = block_scores(
                q_heads,
                pieces[0],
                q_ends,
                pieces[1],
                pieces[2],
                slot_index,
                head_slopes,
                score_scale,
            )[0]
            running_max = jnp.maximum(running[0], jnp.max(scores, axis=-1))
            running_sum = running[1] * jnp.exp(running[0] - running_max) + jnp.sum(
                jnp.exp(scores - running_max[..., None]), axis=-1
            )
            return ((running_max, running_sum), None)

        start_max = jnp.full((head_count, slot_count), -jnp.inf, jnp.float32)
        (top_max, top_sum), _ = lax.scan(
            stats_step, (start_max, jnp.zeros_like(start_max)), (key_heads, key_order, key_ends)
        )
        log_total = top_max + jnp.log(top_sum)

        def out_step(summed, pieces):
            scores = block_scores(
                q_heads,
                pieces[0],
                q_ends,
                pieces[1],
                pieces[2],
                slot_index,
                head_slopes,
                score_scale,
            )[0]
            attn_probs = jnp.exp(scores - log_total[..., None]).astype(jnp.bfloat16)
            return (
                summed
                + jnp.einsum(
                    "hqk,khd->qhd", attn_probs, pieces[3], preferred_element_type=jnp.float32
                ),
                None,
            )

        start_out = jnp.zeros((slot_count, head_count, head_dim), jnp.float32)
        mixed_heads, _ = lax.scan(
            out_step, start_out, (key_heads, key_order, key_ends, value_heads)
        )
        return (mixed_heads, log_total)

    mixed_all, log_totals = lax.map(attend, jnp.arange(seq_count))
    mixed_low = mixed_all.reshape(seq_count, slot_count, model_width).astype(jnp.bfloat16)
    residual = x_float + jnp.einsum(
        "std,de->ste", mixed_low, out_weight, preferred_element_type=jnp.float32
    )
    second_low = layer_norm(residual, second_gain, second_shift).astype(jnp.bfloat16)
    hidden_pre = jnp.einsum(
        "std,df->stf", second_low, hidden_weight, preferred_element_type=jnp.float32
    )
    act_low = jax.nn.gelu(hidden_pre, approximate=False).astype(jnp.bfloat16)
    layer_out = (
        residual
        + jnp.einsum("stf,fd->std", act_low, output_weight, preferred_element_type=jnp.float32)
    ).astype(jnp.bfloat16)
    grad_output_w = jnp.einsum(
        "stf,std->fd", act_low, output_grad, preferred_element_type=jnp.float32
    )
    d_act = jnp.einsum(
        "std,fd->stf", output_grad, output_weight, preferred_element_type=jnp.float32
    )
    _, gelu_pull = jax.vjp(lambda inner: jax.nn.gelu(inner, approximate=False), hidden_pre)
    d_pre_low = gelu_pull(d_act)[0].astype(jnp.bfloat16)
    grad_hidden_w = jnp.einsum(
        "std,stf->df", second_low, d_pre_low, preferred_element_type=jnp.float32
    )
    d_second = jnp.einsum(
        "stf,df->std", d_pre_low, hidden_weight, preferred_element_type=jnp.float32
    )
    _, second_pull = jax.vjp(layer_norm, residual, second_gain, second_shift)
    d_resid_norm, grad_second_g, grad_second_b = second_pull(d_second)
    d_residual = d_resid_norm + output_grad.astype(jnp.float32)
    d_branch = d_residual.astype(jnp.bfloat16)
    grad_out_w = jnp.einsum("std,ste->de", mixed_low, d_branch, preferred_element_type=jnp.float32)
    d_mixed = jnp.einsum(
        "ste,de->std", d_branch, out_weight, preferred_element_type=jnp.float32
    ).astype(jnp.bfloat16)
    d_mixed_heads = d_mixed.reshape(seq_count, slot_count, head_count, head_dim)

    def query_side(seq_index):
        key_heads, value_heads, key_order, key_ends = pick(seq_index)
        q_heads = lax.dynamic_index_in_dim(query_heads, seq_index, 0, keepdims=False)
        q_ends = lax.dynamic_index_in_dim(segment_ends, seq_index, 0, keepdims=False)
        d_heads = lax.dynamic_index_in_dim(d_mixed_heads, seq_index, 0, keepdims=False)
        log_total = lax.dynamic_index_in_dim(log_totals, seq_index, 0, keepdims=False)

        def probs_of(key_block, order_block, ends_block, value_block):
            scores, distance = block_scores(
                q_heads,
                key_block,
                q_ends,
                order_block,
                ends_block,
                slot_index,
                head_slopes,
                score_scale,
            )
            attn_probs = jnp.exp(scores - log_total[..., None])
            d_probs = jnp.einsum(
                "qhd,khd->hqk", d_heads, value_block, preferred_element_type=jnp.float32
            )
            return (attn_probs, d_probs, distance)

        def delta_step(summed, pieces):
            attn_probs, d_probs, _ = probs_of(pieces[0], pieces[1], pieces[2], pieces[3])
            return (summed + jnp.sum(attn_probs * d_probs, axis=-1), None)

        delta_rows, _ = lax.scan(
            delta_step,
            jnp.zeros((head_count, slot_count), jnp.float32),
            (key_heads, key_order, key_ends, value_heads),
        )

        def grad_step(running, pieces):
            attn_probs, d_probs, distance = probs_of(pieces[0], pieces[1], pieces[2], pieces[3])
            d_scores = (attn_probs * (d_probs - delta_rows[..., None])).astype(jnp.bfloat16)
            d_query = running[0] + jnp.einsum(
                "hqk,khd->qhd", d_scores, pieces[0], preferred_element_type=jnp.float32
            )
            d_slopes = running[1] - jnp.sum(
                d_scores.astype(jnp.float32) * distance[None], axis=(1, 2)
            )
            return ((d_query, d_slopes), None)

        start_grads = (
            jnp.zeros((slot_count, head_count, head_dim), jnp.float32),
            jnp.zeros((head_count,), jnp.float32),
        )
        (d_query, d_slopes), _ = lax.scan(
            grad_step, start_grads, (key_heads, key_order, key_ends, value_heads)
        )
        return (d_query * score_scale, delta_rows, d_slopes)

    d_query_all, delta_all, slope_parts = lax.map(query_side, jnp.arange(seq_count))
    grad_slopes = jnp.sum(slope_parts, axis=0)
    d_query_low = d_query_all.reshape(seq_count, slot_count, model_width).astype(jnp.bfloat16)

    def pair_terms(
        pair_rows, order_block, ends_block, q_heads, q_ends, q_index, d_heads, log_total, delta_rows
    ):
        key_block = pair_rows[:, :model_width].reshape(key_rows, head_count, head_dim)
        value_block = pair_rows[:, model_width:].reshape(key_rows, head_count, head_dim)
        scores, _ = block_scores(
            q_heads, key_block, q_ends, order_block, ends_block, q_index, head_slopes, score_scale
        )
        attn_probs = jnp.exp(scores - log_total[..., None])
        d_probs = jnp.einsum(
            "qhd,khd->hqk", d_heads, value_block, preferred_element_type=jnp.float32
        )
        d_scores = (attn_probs * (d_probs - delta_rows[..., None])).astype(jnp.bfloat16)
        d_value = jnp.einsum(
            "hqk,qhd->khd",
            attn_probs.astype(jnp.bfloat16),
            d_heads,
            preferred_element_type=jnp.float32,
        )
        d_key = (
            jnp.einsum("hqk,qhd->khd", d_scores, q_heads, preferred_element_type=jnp.float32)
            * score_scale
        )
        return jnp.concatenate(
            [d_key.reshape(key_rows, model_width), d_value.reshape(key_rows, model_width)], axis=1
        )

    def one_block(block_index):
        offset = block_index * key_rows
        pair_block = lax.dynamic_slice_in_dim(all_pairs, offset, key_rows, 0)
        meta_block = lax.dynamic_slice_in_dim(all_meta, offset, key_rows, 2)
        return jax.vmap(pair_terms, in_axes=(1, 0, 0, 0, 0, None, 0, 0, 0), out_axes=1)(
            pair_block,
            meta_block[0],
            meta_block[1],
            query_heads,
            segment_ends,
            slot_index,
            d_mixed_heads,
            log_totals,
            delta_all,
        )

    pieces = lax.map(one_block, jnp.arange(lax.axis_size("blk") * key_rows // key_rows))
    pair_grads = lax.psum_scatter(
        pieces.reshape(lax.axis_size("blk") * key_rows, seq_count, 2 * model_width).astype(
            jnp.bfloat16
        ),
        "blk",
        scatter_dimension=0,
        tiled=True,
    )
    grad_pair_w = jnp.einsum(
        "srd,rse->de", key_input, pair_grads, preferred_element_type=jnp.float32
    )
    grad_key_w = grad_pair_w[:, :model_width]
    grad_value_w = grad_pair_w[:, model_width:]
    d_key_input = jnp.einsum(
        "rse,de->srd", pair_grads, pair_weight, preferred_element_type=jnp.float32
    )
    grad_query_w = jnp.einsum(
        "std,ste->de", normed, d_query_low, preferred_element_type=jnp.float32
    )
    d_normed = (
        jnp.einsum("ste,de->std", d_query_low, query_weight, preferred_element_type=jnp.float32)
        + d_key_input[:, mem_count:]
    )
    _, first_pull = jax.vjp(layer_norm, x_float, first_gain, first_shift)
    d_tokens, gain_slots, shift_slots = first_pull(d_normed)
    _, mem_pull = jax.vjp(
        lambda gain, shift: layer_norm(mem_float, gain, shift), first_gain, first_shift
    )
    gain_mem, shift_mem = mem_pull(d_key_input[:, :mem_count])
    input_grad = (d_tokens + d_residual).astype(jnp.bfloat16)
    grad_first_g = gain_slots + gain_mem
    grad_first_b = shift_slots + shift_mem
    summed = lax.psum(
        (
            grad_first_g,
            grad_first_b,
            grad_query_w,
            grad_key_w,
            grad_value_w,
            grad_out_w,
            grad_slopes,
            grad_second_g,
            grad_second_b,
            grad_hidden_w,
            grad_output_w,
        ),
        ("seq", "blk"),
    )
    return (
        layer_out,
        input_grad,
        summed[0],
        summed[1],
        summed[2],
        summed[3],
        summed[4],
        summed[5],
        summed[6],
        summed[7],
        summed[8],
        summed[9],
        summed[10],
    )


def solution(mesh):
    placed = (
        P("seq", "blk", None),
        P("seq", "blk", None),
        P("seq", "blk"),
        P("seq", "blk"),
        P("seq"),
        P("seq"),
        P(),
        P(),
        P(),
        P(),
        P(),
        P(),
        P(),
        P(),
        P(),
        P(),
        P(),
        P("seq", "blk", None),
    )
    return jax.shard_map(
        per_device,
        mesh=mesh,
        in_specs=placed,
        out_specs=(
            P("seq", "blk", None),
            P("seq", "blk", None),
            P(),
            P(),
            P(),
            P(),
            P(),
            P(),
            P(),
            P(),
            P(),
            P(),
            P(),
        ),
        check_vma=False,
    )
```

profile of v0, /device:TPU:0, one launch (start us, length us, event | category | flops | bytes accessed | tf_op | source)
XLA Modules:
  0.0 937.0 jit_solution(17816046465124142338)
XLA Ops:
  34.2 73.6 %all-gather.2.cloned.1.call-done = bf16[1536,2,1024]{0,2,1:T(8,128)(2,1)} async-done(((bf16[768,2,1024]{0,2,1:T(8,128)(2,1)}), bf16[1536,2,1024]{0,2,1:T(8,128)(2,1)}) %all-gather.2.cloned.1.call-update) | async-done | bytes 6291472 | tf_op jit(solution)/shard_map/all_gather | solution.py:86
  110.0 168.6 %while.93 = (s32[]{:T(128)}, bf16[2,512,8,64]{1,3,2,0:T(8,128)(2,1)}, f32[2,8,512]{2,1,0:T(8,128)}, s32[2]{0:T(128)}, bf16[1536,2,1024]{0,2,1:T(8,128)(2,1)}, /*...) while((s32[]{:T(128)}, ...), condition=%wide.region_11.12_spmd.clone, body=%wide.region_4.11_spmd.clone.sunk | while | flops 1264345600 | bytes 82579288 | solution.py:157
  138.2 21.8 %while.98 = (s32[]{:T(128)}, f32[8,512]{1,0:T(8,128)S(1)}, f32[8,512]{1,0:T(8,128)S(1)}, s32[2,768]{1,0:T(2,128)S(1)}, s32[512]{0:T(512)S(1)}, /*index=5*/bf16[2...) while((s32[]{:T(128)}, f32[8,512]{1,0:T(8,128)S(1)}, ...), condition=%wide.region_8.8_spmd.clone, body=%wide.region_5.7_spmd.clone.sunk | while | flops 438456320 | bytes 32610988 | solution.py:126
  160.6 31.5 %while.99 = (s32[]{:T(128)}, f32[512,8,64]{0,2,1:T(8,128)}, bf16[2,768,8,64]{1,3,2,0:T(8,128)(2,1)}, s32[2,768]{1,0:T(2,128)S(1)}, s32[512]{0:T(512)S(1)}, /*ind...) while((s32[]{:T(128)}, f32[512,8,64]{0,2,1:T(8,128)}, ...), condition=%wide.region_10.10_spmd.clone, body=%wide.region_9.9_spmd.clone.sunk | while | flops 825884672 | bytes 19438292 | solution.py:152
  167.3 8.0 fusion.238
  183.1 8.1 fusion.238
  222.2 21.8 %while.98 = (s32[]{:T(128)}, f32[8,512]{1,0:T(8,128)S(1)}, f32[8,512]{1,0:T(8,128)S(1)}, s32[2,768]{1,0:T(2,128)S(1)}, s32[512]{0:T(512)S(1)}, /*index=5*/bf16[2...) while((s32[]{:T(128)}, f32[8,512]{1,0:T(8,128)S(1)}, ...), condition=%wide.region_8.8_spmd.clone, body=%wide.region_5.7_spmd.clone.sunk | while | flops 438456320 | bytes 32610988 | solution.py:126
  244.6 31.5 %while.99 = (s32[]{:T(128)}, f32[512,8,64]{0,2,1:T(8,128)}, bf16[2,768,8,64]{1,3,2,0:T(8,128)(2,1)}, s32[2,768]{1,0:T(2,128)S(1)}, s32[512]{0:T(512)S(1)}, /*ind...) while((s32[]{:T(128)}, f32[512,8,64]{0,2,1:T(8,128)}, ...), condition=%wide.region_10.10_spmd.clone, body=%wide.region_9.9_spmd.clone.sunk | while | flops 825884672 | bytes 19438292 | solution.py:152
  251.3 8.1 fusion.238
  267.1 8.1 fusion.238
  285.9 20.1 %multiply_convert_fusion = (bf16[2,512,2048]{2,1,0:T(8,128)(2,1)}, f32[2,512,2048]{2,1,0:T(8,128)}) fusion(f32[2,512,2048]{2,1,0:T(8,128)S(1)} %get-tuple-element.1058, u8[512,2048]{1,0:T(8,128)(4,1)S(1)} %get-tuple-element.841, u8[512,2048]{1,0:T(8,128)(4,1)S(1)} %get-tuple-element.840), kind=kLoop, calls=%fused_computation.134 | loop fusion | flops 146800640 | bytes 23068672 | tf_op jit(solution)/shard_map/convert_element_type | solution.py:166
  306.0 6.8 add_convert_fusion
  322.5 155.2 %while.96 = (s32[]{:T(128)}, bf16[2,512,8,64]{1,3,2,0:T(8,128)(2,1)}, f32[2,8,512]{2,1,0:T(8,128)}, f32[2,8]{1,0:T(2,128)}, s32[2]{0:T(128)}, /*index=5*/bf16[15...) while((s32[]{:T(128)}, ...), condition=%wide.region_23.24_spmd.clone, body=%wide.region_16.23_spmd.clone.sunk | while | flops 2073039360 | bytes 125587736 | solution.py:249
  357.9 18.1 %while.100 = (s32[]{:T(128)}, f32[8,512]{1,0:T(8,128)S(1)}, s32[2,768]{1,0:T(2,128)S(1)}, s32[512]{0:T(512)S(1)}, bf16[2,768,8,64]{1,3,2,0:T(8,128)(2,1)S(1)}, /...) while((s32[]{:T(128)}, f32[8,512]{1,0:T(8,128)S(1)}, ...), condition=%wide.region_19.19_spmd.clone, body=%wide.region_17.18_spmd.clone.sunk | while | flops 828510208 | bytes 40212728 | solution.py:223
  376.0 23.0 %while.101 = (s32[]{:T(128)}, f32[512,8,64]{0,2,1:T(8,128)S(1)}, f32[8]{0:T(128)S(1)}, bf16[2,768,8,64]{1,3,2,0:T(8,128)(2,1)S(1)}, s32[2,768]{1,0:T(2,128)S(1)}...) while((s32[]{:T(128)}, f32[512,8,64]{0,2,1:T(8,128)S(1)}, ...), condition=%wide.region_22.22_spmd.clone, body=%wide.region_20.21_spmd.clone.sunk | while | flops 1244266496 | bytes 49339216 | solution.py:244
  378.4 7.8 multiply_reduce_fusion.5
  389.9 7.8 multiply_reduce_fusion.5
  435.2 18.1 %while.100 = (s32[]{:T(128)}, f32[8,512]{1,0:T(8,128)S(1)}, s32[2,768]{1,0:T(2,128)S(1)}, s32[512]{0:T(512)S(1)}, bf16[2,768,8,64]{1,3,2,0:T(8,128)(2,1)S(1)}, /...) while((s32[]{:T(128)}, f32[8,512]{1,0:T(8,128)S(1)}, ...), condition=%wide.region_19.19_spmd.clone, body=%wide.region_17.18_spmd.clone.sunk | while | flops 828510208 | bytes 40212728 | solution.py:223
  437.6 6.6 fusion.222
  453.3 23.0 %while.101 = (s32[]{:T(128)}, f32[512,8,64]{0,2,1:T(8,128)S(1)}, f32[8]{0:T(128)S(1)}, bf16[2,768,8,64]{1,3,2,0:T(8,128)(2,1)S(1)}, s32[2,768]{1,0:T(2,128)S(1)}...) while((s32[]{:T(128)}, f32[512,8,64]{0,2,1:T(8,128)S(1)}, ...), condition=%wide.region_22.22_spmd.clone, body=%wide.region_20.21_spmd.clone.sunk | while | flops 1244266496 | bytes 49339216 | solution.py:244
  455.7 7.8 multiply_reduce_fusion.5
  467.2 7.8 multiply_reduce_fusion.5
  477.7 116.6 %while.97 = (s32[]{:T(128)}, bf16[2,768,2,1024]{3,1,0,2:T(8,128)(2,1)}, s32[2]{0:T(128)S(1)}, s32[2,2,1536]{2,1,0:T(2,128)}, bf16[1536,2,1024]{0,2,1:T(8,128)(2,...) while((s32[]{:T(128)}, ...), condition=%wide.region_25.26_spmd.clone, body=%wide.region_24.25_spmd.clone.sunk | while | flops 3319529984 | bytes 129511832 | solution.py:296
  485.4 11.3 %fusion.214 = f32[2,8,768,512]{3,2,1,0:T(8,128)} fusion(bf16[2,768,8,64]{1,3,2,0:T(8,128)(2,1)S(1)} %bitcast.354, bf16[2,512,8,64]{1,3,2,0:T(8,128)(2,1)} %get-tuple-element.2049), kind=kOutput, calls=%fused_computation.237.clone.1 | convolution fusion | flops 805306368 | bytes 27787264 | tf_op jit(solution)/shard_map/while/body/eval_jaxpr/vmap(qhd,khd->hqk)/dot_general | solution.py:22
  496.7 19.0 %fusion.216 = bf16[2,8,768,64]{2,3,1,0:T(8,128)(2,1)} fusion(bf16[2,512,8,64]{1,3,2,0:T(8,128)(2,1)} %get-tuple-element.2049, f32[2,8,768,512]{3,2,1,0:T(8,128)} %fusion.214, f32[2,8,512]{2,1,0:T(8,128)S(1)} %copy-done.60, f32[2,8,512]{2,1,0:T(8,128)} %get-tuple-element.2052, f32[2,512,768]{1,2,0:T(8,128)S(1)} %subtract_convert_fusion.10, ...), kind=kOutput, calls=%fused_computation.15.clone.1 | convolution fusion | flops 1662517248 | bytes 34406432 | tf_op jit(solution)/shard_map/while/body/eval_jaxpr/vmap(hqk,qhd->khd)/dot_general | solution.py:273
  515.7 13.2 %fusion.215 = bf16[2,8,768,64]{2,3,1,0:T(8,128)(2,1)S(1)} fusion(bf16[2,512,8,64]{1,3,2,0:T(8,128)(2,1)} %get-tuple-element.2053, f32[2,8,768,512]{3,2,1,0:T(8,128)} %fusion.214, f32[2,8,512]{2,1,0:T(8,128)} %get-tuple-element.2052, f32[2,512,768]{1,2,0:T(8,128)S(1)} %subtract_convert_fusion.10, f32[8]{0:T(128)} %get-tuple-element.2050, ...), kind=kOutput, calls=%fused_computation.10.clone.1 | convolution fusion | flops 843055104 | bytes 31752224 | tf_op jit(solution)/shard_map/while/body/eval_jaxpr/vmap(hqk,qhd->khd)/dot_general | solution.py:266
  543.6 11.3 %fusion.214 = f32[2,8,768,512]{3,2,1,0:T(8,128)} fusion(bf16[2,768,8,64]{1,3,2,0:T(8,128)(2,1)S(1)} %bitcast.354, bf16[2,512,8,64]{1,3,2,0:T(8,128)(2,1)} %get-tuple-element.2049), kind=kOutput, calls=%fused_computation.237.clone.1 | convolution fusion | flops 805306368 | bytes 27787264 | tf_op jit(solution)/shard_map/while/body/eval_jaxpr/vmap(qhd,khd->hqk)/dot_general | solution.py:22
  554.9 19.0 %fusion.216 = bf16[2,8,768,64]{2,3,1,0:T(8,128)(2,1)} fusion(bf16[2,512,8,64]{1,3,2,0:T(8,128)(2,1)} %get-tuple-element.2049, f32[2,8,768,512]{3,2,1,0:T(8,128)} %fusion.214, f32[2,8,512]{2,1,0:T(8,128)S(1)} %copy-done.60, f32[2,8,512]{2,1,0:T(8,128)} %get-tuple-element.2052, f32[2,512,768]{1,2,0:T(8,128)S(1)} %subtract_convert_fusion.10, ...), kind=kOutput, calls=%fused_computation.15.clone.1 | convolution fusion | flops 1662517248 | bytes 34406432 | tf_op jit(solution)/shard_map/while/body/eval_jaxpr/vmap(hqk,qhd->khd)/dot_general | solution.py:273
  573.9 13.2 %fusion.215 = bf16[2,8,768,64]{2,3,1,0:T(8,128)(2,1)S(1)} fusion(bf16[2,512,8,64]{1,3,2,0:T(8,128)(2,1)} %get-tuple-element.2053, f32[2,8,768,512]{3,2,1,0:T(8,128)} %fusion.214, f32[2,8,512]{2,1,0:T(8,128)} %get-tuple-element.2052, f32[2,512,768]{1,2,0:T(8,128)S(1)} %subtract_convert_fusion.10, f32[8]{0:T(128)} %get-tuple-element.2050, ...), kind=kOutput, calls=%fused_computation.10.clone.1 | convolution fusion | flops 843055104 | bytes 31752224 | tf_op jit(solution)/shard_map/while/body/eval_jaxpr/vmap(hqk,qhd->khd)/dot_general | solution.py:266
  609.9 61.7 %reduce-scatter.2.cloned.1.call-done = bf16[768,2,1024]{2,0,1:T(8,128)(2,1)} async-done(((bf16[1536,2,1024]{2,0,1:T(8,128)(2,1)}), bf16[768,2,1024]{2,0,1:T(8,128)(2,1)}) %reduce-scatter.2.cloned.1.call-update) | async-done | bytes 3145744 | tf_op jit(solution)/shard_map/reduce_scatter | solution.py:297
  690.4 40.9 %all-reduce = (f32[512]{0:T(512)}, f32[512]{0:T(512)}, f32[8]{0:T(128)}, f32[512]{0:T(512)}, f32[512]{0:T(512)}) all-reduce(f32[512]{0:T(512)S(1)} %add.197, f32[512]{0:T(512)S(1)} %add.198, f32[8]{0:T(128)S(1)} %reduce_sum.201, f32[512]{0:T(512)S(1)} %copy-done.65, ...), channel_id=1, replica_groups=mesh['seq'=16,'blk'=2] {'seq','blk'}, use_global_device_ids=true, to_apply=%region_31.32 | all-reduce | flops 2056 | bytes 16448 | tf_op jit(solution)/shard_map/psum | solution.py:329
  734.5 183.3 %all-reduce.4.cloned.1.call-done = (f32[512,512]{1,0:T(8,128)}, f32[512,512]{1,0:T(8,128)}, f32[512,512]{1,0:T(8,128)}, f32[512,512]{1,0:T(8,128)}, f32[512,2048]{1,0:T(8,128)}, /*index=5*/f32[2048,512]{1,0:T(8,128)}) async-done(((f32[512,512]{1,0:T(8,128)}, f32[512,512]{1,0:T(8,128)}, f32[512,512]{1,0:T(8,128)}, f32[512,512]{1,0:T(8,128)}, f32[512,2048]{1,0:T(8,128)}, /*index=5*/f32[2048,512]{1,0:T(8,128)}), ...) | async-done | bytes 12582928 | tf_op jit(solution)/shard_map/psum | solution.py:329
  (456 shorter events, 367.0 us)
Async XLA Ops:
  7.2 274.4 %copy-start = (bf16[512,2048]{1,0:T(8,128)(2,1)S(1)}, bf16[512,2048]{1,0:T(8,128)(2,1)}, u32[]{:S(2)}) copy-start(bf16[512,2048]{1,0:T(8,128)(2,1)} %param.47) | copy-start | bytes 6291460
  7.2 12.1 %copy-start.2 = (bf16[2,512,512]{2,1,0:T(8,128)(2,1)S(1)}, bf16[2,512,512]{2,1,0:T(8,128)(2,1)}, u32[]{:S(2)}) copy-start(bf16[2,512,512]{2,1,0:T(8,128)(2,1)} %param.32) | copy-start | bytes 3145732
  7.2 10.6 %copy-start.48 = (f32[512]{0:T(512)S(1)}, f32[512]{0:T(512)}, u32[]{:S(2)}) copy-start(f32[512]{0:T(512)} %param.38) | copy-start | bytes 6148
  7.2 10.6 %copy-start.63 = (f32[512]{0:T(512)S(1)}, f32[512]{0:T(512)}, u32[]{:S(2)}) copy-start(f32[512]{0:T(512)} %param.39) | copy-start | bytes 6148
  7.2 100.6 %all-gather.2.cloned.1.call-start = ((), (), s32[]{:S(2)}) async-start(), calls=%async_computation.1 | async-start | bytes 9437184 | tf_op jit(solution)/shard_map/all_gather | solution.py:86
  8.6 11.1 %copy-start.56 = (f32[2,256]{1,0:T(2,128)}, f32[2,256]{1,0:T(2,128)S(1)}, u32[]{:S(2)}) copy-start(f32[2,256]{1,0:T(2,128)S(1)} %broadcast_multiply_fusion.2) | copy-start | bytes 6148
  10.0 9.8 %copy-start.61 = (f32[2,256]{1,0:T(2,128)}, f32[2,256]{1,0:T(2,128)S(1)}, u32[]{:S(2)}) copy-start(f32[2,256]{1,0:T(2,128)S(1)} %add_rsqrt_fusion) | copy-start | bytes 6148
  11.5 8.3 copy-start.38
  13.7 10.8 %copy-start.44 = (f32[2,512]{1,0:T(2,128)}, f32[2,512]{1,0:T(2,128)S(1)}, u32[]{:S(2)}) copy-start(f32[2,512]{1,0:T(2,128)S(1)} %fusion.125) | copy-start | bytes 12292
  24.5 6.9 copy-start.28
  24.6 647.0 %reduce-scatter.2.cloned.1.call-start = ((), (), s32[]{:S(2)}) async-start(), calls=%async_computation.2 | async-start | bytes 9437184 | tf_op jit(solution)/shard_map/reduce_scatter | solution.py:297
  160.6 6.7 copy-start.8
  176.3 6.7 copy-start.8
  244.6 6.7 copy-start.8
  260.4 6.7 copy-start.8
  281.2 35.2 %copy-start.4 = (f32[2,512,512]{2,1,0:T(8,128)}, f32[2,512,512]{2,1,0:T(8,128)S(1)}, u32[]{:S(2)}) copy-start(f32[2,512,512]{2,1,0:T(8,128)S(1)} %get-tuple-element.1057) | copy-start | bytes 6291460
  281.2 35.2 %copy-start.40 = (f32[2,512]{1,0:T(2,128)}, f32[2,512]{1,0:T(2,128)S(1)}, u32[]{:S(2)}) copy-start(f32[2,512]{1,0:T(2,128)S(1)} %broadcast_multiply_fusion) | copy-start | bytes 12292
  281.6 34.7 %copy-start.42 = (f32[2,512]{1,0:T(2,128)}, f32[2,512]{1,0:T(2,128)S(1)}, u32[]{:S(2)}) copy-start(f32[2,512]{1,0:T(2,128)S(1)} %fusion.126) | copy-start | bytes 12292
  285.9 20.2 %copy-start.23 = (bf16[2,512,512]{2,1,0:T(8,128)(2,1)S(1)}, bf16[2,512,512]{2,1,0:T(8,128)(2,1)}, u32[]{:S(2)}) copy-start(bf16[2,512,512]{2,1,0:T(8,128)(2,1)} %param.49) | copy-start | bytes 3145732
  285.9 20.2 %copy-start.72 = (bf16[2048,512]{1,0:T(8,128)(2,1)S(1)}, bf16[2048,512]{1,0:T(8,128)(2,1)}, u32[]{:S(2)}) copy-start(bf16[2048,512]{1,0:T(8,128)(2,1)} %param.48) | copy-start | bytes 6291460
  375.9 23.1 %copy-start.67 = (f32[2,8]{1,0:T(2,128)S(1)}, f32[2,8]{1,0:T(2,128)}, u32[]{:S(2)}) copy-start(f32[2,8]{1,0:T(2,128)} %get-tuple-element.1969) | copy-start | bytes 196 | tf_op jit(solution)/shard_map/while
  376.0 23.1 %copy-start.58 = (f32[2,8,512]{2,1,0:T(8,128)S(1)}, f32[2,8,512]{2,1,0:T(8,128)}, u32[]{:S(2)}) copy-start(f32[2,8,512]{2,1,0:T(8,128)} %get-tuple-element.1968) | copy-start | bytes 98308 | tf_op jit(solution)/shard_map/while
  453.3 23.1 %copy-start.67 = (f32[2,8]{1,0:T(2,128)S(1)}, f32[2,8]{1,0:T(2,128)}, u32[]{:S(2)}) copy-start(f32[2,8]{1,0:T(2,128)} %get-tuple-element.1969) | copy-start | bytes 196 | tf_op jit(solution)/shard_map/while
  453.3 23.1 %copy-start.58 = (f32[2,8,512]{2,1,0:T(8,128)S(1)}, f32[2,8,512]{2,1,0:T(8,128)}, u32[]{:S(2)}) copy-start(f32[2,8,512]{2,1,0:T(8,128)} %get-tuple-element.1968) | copy-start | bytes 98308 | tf_op jit(solution)/shard_map/while
  485.4 11.3 %copy-start.60 = (f32[2,8,512]{2,1,0:T(8,128)S(1)}, f32[2,8,512]{2,1,0:T(8,128)}, u32[]{:S(2)}) copy-start(f32[2,8,512]{2,1,0:T(8,128)} %get-tuple-element.2054) | copy-start | bytes 98308 | tf_op jit(solution)/shard_map/while
  515.7 13.2 %copy-start.7 = (bf16[2,8,768,64]{2,3,1,0:T(8,128)(2,1)S(1)}, bf16[2,8,768,64]{2,3,1,0:T(8,128)(2,1)}, u32[]{:S(2)}) copy-start(bf16[2,8,768,64]{2,3,1,0:T(8,128)(2,1)} %fusion.216) | copy-start | bytes 4718596 | tf_op jit(solution)/shard_map/while
  543.6 11.3 %copy-start.60 = (f32[2,8,512]{2,1,0:T(8,128)S(1)}, f32[2,8,512]{2,1,0:T(8,128)}, u32[]{:S(2)}) copy-start(f32[2,8,512]{2,1,0:T(8,128)} %get-tuple-element.2054) | copy-start | bytes 98308 | tf_op jit(solution)/shard_map/while
  573.9 13.2 %copy-start.7 = (bf16[2,8,768,64]{2,3,1,0:T(8,128)(2,1)S(1)}, bf16[2,8,768,64]{2,3,1,0:T(8,128)(2,1)}, u32[]{:S(2)}) copy-start(bf16[2,8,768,64]{2,3,1,0:T(8,128)(2,1)} %fusion.216) | copy-start | bytes 4718596 | tf_op jit(solution)/shard_map/while
  594.4 323.4 %all-reduce.4.cloned.1.call-start = ((), (), s32[]{:S(2)}) async-start(), calls=%async_computation.3 | async-start | bytes 25165824 | tf_op jit(solution)/shard_map/psum | solution.py:329
  678.0 6.3 copy-start.35
  687.9 43.4 %copy-start.11 = (f32[2,512,512]{2,1,0:T(8,128)S(1)}, f32[2,512,512]{2,1,0:T(8,128)}, u32[]{:S(2)}) copy-start(f32[2,512,512]{2,1,0:T(8,128)} %copy-done.10) | copy-start | bytes 6291460
  687.9 43.4 %copy-start.51 = (f32[2,512]{1,0:T(2,128)S(1)}, f32[2,512]{1,0:T(2,128)}, u32[]{:S(2)}) copy-start(f32[2,512]{1,0:T(2,128)} %copy-done.50) | copy-start | bytes 12292
  (66 other events, 165.2 us)
Sparse Core Ops, SparseCore 0:
  24.7 83.0 all-gather.1
  594.5 77.0 reduce-scatter.1
  680.3 237.4 all-reduce.3
where the time goes:
time: 944 us; the launch traced here: 937 us
  waiting for transfers between devices  319 us (34%)
  matrix products  271 us (29%)
  local copies, waits for them, and re-layouts  199 us (21%)
  other arithmetic  75.8 us (8%)
  blocking collectives  46.3 us (5%)
  between operations  14.7 us (2%)
  loops' own time  11.6 us (1%)
    psum x1, waiting for transfers between devices, per_device(): lax.psum((grad_first_g, grad_first_b, grad_query_w, grad_key_w, grad_valu...  183 us
    all_gather x1, waiting for transfers between devices, per_device(): lax.all_gather(key_value, 'blk', axis=0, tiled=True)  73.6 us
    reduce_scatter x1, waiting for transfers between devices, per_device(): lax.psum_scatter(pieces.reshape(lax.axis_size('blk') * key_rows, seq_coun...  61.7 us
    dot_general x14, matrix products, block_scores(): jnp.einsum('qhd,khd->hqk', q_heads, key_block, preferred_element_type=jnp...  58.7 us
    dot_general x8, matrix products, probs_of(): jnp.einsum('qhd,khd->hqk', d_heads, value_block, preferred_element_type=j...  57.9 us
    psum x1, blocking collectives, per_device(): lax.psum((grad_first_g, grad_first_b, grad_query_w, grad_key_w, grad_valu...  40.9 us
    dot_general x2, matrix products, pair_terms(): jnp.einsum('hqk,qhd->khd', d_scores, q_heads, preferred_element_type=jnp....  37.9 us
    dot_general x4, matrix products, out_step(): jnp.einsum('hqk,khd->qhd', attn_probs, pieces[3], preferred_element_type=...  32.2 us
  transfers between devices with their start and end apart: 3, of which 3 were waited for; matrix products, arithmetic and copies ran while one was open for 3% of the time, Pallas kernels for 0%

commit v1 on v0

--- a/solution.py
+++ b/solution.py
@@ -1,12 +1,421 @@
+import functools
 import math
 
 import jax
 import jax.numpy as jnp
 from jax import lax
+from jax.experimental import pallas as pl
+from jax.experimental.pallas import tpu as pltpu
 from jax.sharding import PartitionSpec as P
 
 epsilon = 1e-05
 far_order = 1073741824
+f32 = jnp.float32
+bf16 = jnp.bfloat16
+BLOCK = 256
+LOG2E = 1.4426950408889634
+LN2 = 0.6931471805599453
+
+
+def dot_nn(left, right):
+    return lax.dot_general(left, right, (((1,), (0,)), ((), ())), preferred_element_type=f32)
+
+
+def dot_nt(left, right):
+    return lax.dot_general(left, right, (((1,), (1,)), ((), ())), preferred_element_type=f32)
+
+
+def norm_stats(values):
+    centred = values - jnp.mean(values, axis=-1, keepdims=True)
+    spread = jnp.mean(centred * centred, axis=-1, keepdims=True)
+    scale = lax.rsqrt(spread + epsilon)
+    return centred * scale, scale
+
+
+def norm_back(unit, scale, grad_unit):
+    mean_grad = jnp.mean(grad_unit, axis=-1, keepdims=True)
+    mean_prod = jnp.mean(grad_unit * unit, axis=-1, keepdims=True)
+    return (grad_unit - mean_grad - unit * mean_prod) * scale
+
+
+def pieces_of(value, count):
+    out = []
+    for _ in range(count):
+        part = value.astype(bf16).astype(f32)
+        out.append(part)
+        value = value - part
+    return out
+
+
+ERFC_P = 0.4
+ERFC_C = (0.22567586600780487, 0.2256695181131363, 0.2078438550233841, 0.16853390634059906, 0.1414608359336853, -0.005667657125741243, 0.16915477812290192, -0.18294358253479004, 0.050272583961486816)
+
+
+def gelu_both(x):
+    a = jnp.abs(x) * math.sqrt(0.5)
+    t = 1.0 / (1.0 + ERFC_P * a)
+    poly = jnp.full_like(t, ERFC_C[-1])
+    for c in ERFC_C[-2::-1]:
+        poly = poly * t + c
+    ex = jnp.exp(-0.5 * (x * x))
+    half = 0.5 * (poly * t * ex)
+    cdf = jnp.where(x >= 0, 1.0 - half, half)
+    return x * cdf, cdf + x * ex * (1.0 / math.sqrt(2.0 * math.pi))
+
+
+def col_sum8(value):
+    return jnp.sum(value.reshape(-1, 8, value.shape[-1]), axis=0)
+
+
+def layer_kernel(
+    counts_ref,
+    lengths_ref,
+    which_ref,
+    x_ref,
+    mem_ref,
+    ends_ref,
+    og_ref,
+    gain1_ref,
+    shift1_ref,
+    wq_ref,
+    wk_ref,
+    wv_ref,
+    wo_ref,
+    slopes_ref,
+    gain2_ref,
+    shift2_ref,
+    w1_ref,
+    w2_ref,
+    layer_ref,
+    ingrad_ref,
+    gq_ref,
+    gk_ref,
+    gv_ref,
+    go_ref,
+    gw1_ref,
+    gw2t_ref,
+    small_ref,
+    keyint,
+    k_s,
+    v_s,
+    kx,
+    q_s,
+    qt,
+    rl_s,
+    o_s,
+    mixed,
+    gw1_s,
+    gw2t_s,
+    go_s,
+    dres,
+    dolt,
+    delta_s,
+    *probs,
+):
+    S, D = x_ref.shape
+    M = mem_ref.shape[0]
+    R = M + S
+    FF = w1_ref.shape[1]
+    H = slopes_ref.shape[0]
+    DH = D // H
+    HP = H // 2
+    NB = S // BLOCK
+    MB = M // BLOCK
+    which = which_ref[0]
+    count = counts_ref[which]
+    length = lengths_ref[which]
+    gain1 = gain1_ref[...]
+    shift1 = shift1_ref[...]
+    gain2 = gain2_ref[...]
+    shift2 = shift2_ref[...]
+
+    lane = lax.broadcasted_iota(jnp.int32, (128, 128), 1)
+    row = lax.broadcasted_iota(jnp.int32, (128, 128), 0)
+    for r in range(R // 128):
+        ends = ends_ref[:, r * 128 : (r + 1) * 128].astype(f32)
+        end_col = jnp.broadcast_to(ends, (128, 128)).T
+        high = jnp.floor(end_col * (1.0 / 256.0)) * 256.0
+        index = row + r * 128
+        if r * 128 < M:
+            valid = index >= M - length
+        else:
+            valid = index - M < count
+        bias = jnp.where(valid, 0.0, -1e30)
+        extra = jnp.where(lane < 3, high, jnp.where(lane < 6, end_col - high, bias))
+        extra = jnp.where(lane == 7, 1.0, jnp.where(lane > 7, 0.0, extra))
+        kx[r * 128 : (r + 1) * 128, :] = extra.astype(bf16)
+
+    def project(normed, key_rows):
+        keyint[:, key_rows] = normed.T
+        k_s[key_rows, :] = dot_nn(normed, wk_ref[...]).astype(bf16)
+        v_s[key_rows, :] = dot_nn(normed, wv_ref[...]).astype(bf16)
+
+    def norm_mem(b, _):
+        rows = pl.ds(pl.multiple_of(b * BLOCK, BLOCK), BLOCK)
+        unit, _ = norm_stats(mem_ref[rows, :].astype(f32))
+        project((unit * gain1 + shift1).astype(bf16), rows)
+        return 0
+
+    def norm_slot(b, _):
+        rows = pl.ds(pl.multiple_of(b * BLOCK, BLOCK), BLOCK)
+        key_rows = pl.ds(pl.multiple_of(b * BLOCK + M, BLOCK), BLOCK)
+        unit, _ = norm_stats(x_ref[rows, :].astype(f32))
+        normed = (unit * gain1 + shift1).astype(bf16)
+        project(normed, key_rows)
+        query = (dot_nn(normed, wq_ref[...]) * (LOG2E / math.sqrt(DH))).astype(bf16)
+        q_s[rows, :] = query
+        qt[:, rows] = query.T
+        return 0
+
+    lax.fori_loop(0, MB, norm_mem, 0)
+    lax.fori_loop(0, NB, norm_slot, 0)
+
+    lane_q = lax.broadcasted_iota(jnp.int32, (BLOCK, 128), 1)
+    first_half = lane_q < DH
+    lane_row = lax.broadcasted_iota(jnp.int32, (1, 128), 1)
+
+    def key_full(lanes, keys):
+        return jnp.concatenate([k_s[0:keys, lanes], kx[0:keys, :]], axis=1)
+
+    def value_full(lanes, keys):
+        return jnp.concatenate([v_s[0:keys, lanes], jnp.ones((keys, 128), bf16)], axis=1)
+
+    def query_extra(head):
+        slope = jnp.full((1, 128), slopes_ref[head] * LOG2E, f32)
+        s1, s2, s3 = pieces_of(slope, 3)
+        at = jnp.where(lane_row >= 3, lane_row - 3, lane_row)
+        out = jnp.where(at == 0, s1, jnp.where(at == 1, s2, s3))
+        out = jnp.where(lane_row < 6, out, jnp.where(lane_row == 6, 1.0, 0.0))
+        return out
+
+    rl_s[...] = jnp.zeros_like(rl_s)
+    for b in range(NB):
+        keys = M + (b + 1) * BLOCK
+        rows = slice(b * BLOCK, (b + 1) * BLOCK)
+        e_ref = probs[b]
+
+        def fwd_pair(p, _):
+            lanes = pl.ds(pl.multiple_of(p * 128, 128), 128)
+            q_pair = q_s[rows, lanes]
+            outs = []
+            for half in range(2):
+                keep = first_half if half == 0 else jnp.logical_not(first_half)
+                q_half = jnp.where(keep, q_pair, jnp.zeros_like(q_pair))
+                extra = jnp.broadcast_to(query_extra(2 * p + half), (BLOCK, 128)).astype(bf16)
+                q_full = jnp.concatenate([q_half, extra], axis=1)
+                scores = dot_nt(q_full, key_full(lanes, keys))
+                diag = scores[:, keys - BLOCK :]
+                below = lax.broadcasted_iota(
+                    jnp.int32, (BLOCK, BLOCK), 1
+                ) <= lax.broadcasted_iota(jnp.int32, (BLOCK, BLOCK), 0)
+                diag = jnp.where(below, diag, -1e30)
+                scores = jnp.concatenate([scores[:, : keys - BLOCK], diag], axis=1)
+                top = jnp.max(scores, axis=1, keepdims=True)
+                e = jnp.exp2(scores - top).astype(bf16)
+                e_ref[2 * p + half, :, :] = e
+                both = dot_nn(e, value_full(lanes, keys))
+                outs.append((both[:, 0:128], 1.0 / both[:, 128:256]))
+            rl = jnp.where(first_half, outs[0][1], outs[1][1])
+            o = jnp.where(first_half, outs[0][0], outs[1][0]) * rl
+            packed = jnp.where(lane_q == 2 * p, outs[0][1], rl_s[rows, :])
+            rl_s[rows, :] = jnp.where(lane_q == 2 * p + 1, outs[1][1], packed)
+            o_s[rows, lanes] = o
+            mixed[rows, lanes] = o.astype(bf16)
+            return 0
+
+        lax.fori_loop(0, HP, fwd_pair, 0)
+
+    gw1_s[...] = jnp.zeros_like(gw1_s)
+    gw2t_s[...] = jnp.zeros_like(gw2t_s)
+    go_s[...] = jnp.zeros_like(go_s)
+    CH = 512
+
+    def feed(b, sums):
+        rows = pl.ds(pl.multiple_of(b * BLOCK, BLOCK), BLOCK)
+        mix = mixed[rows, :]
+        residual = x_ref[rows, :].astype(f32) + dot_nn(mix, wo_ref[...])
+        unit, scale = norm_stats(residual)
+        second = (unit * gain2 + shift2).astype(bf16)
+        second_t = second.T
+        og = og_ref[rows, :]
+        og_t = og.T
+        out = residual
+        d_second = jnp.zeros((BLOCK, D), f32)
+        for c in range(FF // CH):
+            cols = slice(c * CH, (c + 1) * CH)
+            hidden = dot_nn(second, w1_ref[:, cols])
+            d_act = dot_nt(og, w2_ref[cols, :])
+            act, slope = gelu_both(hidden)
+            act = act.astype(bf16)
+            d_pre = (d_act * slope).astype(bf16)
+            out = out + dot_nn(act, w2_ref[cols, :])
+            d_second = d_second + dot_nt(d_pre, w1_ref[:, cols])
+            gw2t_s[:, cols] += dot_nn(og_t, act)
+            gw1_s[:, cols] += dot_nn(second_t, d_pre)
+        layer_ref[rows, :] = out.astype(bf16)
+        d_residual = og.astype(f32) + norm_back(unit, scale, d_second * gain2)
+        dres[rows, :] = d_residual
+        d_branch = d_residual.astype(bf16)
+        go_s[...] += dot_nn(mix.T, d_branch)
+        d_mixed = dot_nt(d_branch, wo_ref[...]).astype(bf16).astype(f32)
+        rl_b = rl_s[rows, :]
+        rl_wide = []
+        for p in range(HP):
+            first = jnp.broadcast_to(rl_b[:, 2 * p : 2 * p + 1], (BLOCK, 128))
+            other = jnp.broadcast_to(rl_b[:, 2 * p + 1 : 2 * p + 2], (BLOCK, 128))
+            rl_wide.append(jnp.where(first_half, first, other))
+        dol_b = (d_mixed * jnp.concatenate(rl_wide, axis=1)).astype(bf16)
+        mixed[rows, :] = dol_b
+        dolt[:, rows] = dol_b.T
+        prod = dol_b.astype(f32) * o_s[rows, :]
+        packed = jnp.zeros((BLOCK, 128), f32)
+        for head in range(H):
+            part = prod[:, (head // 2) * 128 : (head // 2 + 1) * 128]
+            keep = first_half if head % 2 == 0 else jnp.logical_not(first_half)
+            delta = jnp.sum(jnp.where(keep, part, 0.0), axis=1, keepdims=True)
+            for at, piece in enumerate(pieces_of(jnp.broadcast_to(-delta, (BLOCK, 128)), 3)):
+                packed = jnp.where(lane_q == 4 * head + at, piece, packed)
+        delta_s[rows, :] = packed.astype(bf16)
+        return sums[0] + col_sum8(d_second * unit), sums[1] + col_sum8(d_second)
+
+    zero8 = jnp.zeros((8, D), f32)
+    gain2_sum, shift2_sum = lax.fori_loop(0, NB, feed, (zero8, zero8))
+    gw1_ref[...] = gw1_s[...].astype(bf16)
+    gw2t_ref[...] = gw2t_s[...].astype(bf16)
+    go_ref[...] = go_s[...].astype(bf16)
+
+    dkt, dvt = gw1_s.at[:, 0:R], gw2t_s.at[:, 0:R]
+    dkt[...] = jnp.zeros((D, R), f32)
+    dvt[...] = jnp.zeros((D, R), f32)
+    small_ref[...] = jnp.zeros_like(small_ref)
+    for b in range(NB):
+        keys = M + (b + 1) * BLOCK
+        rows = slice(b * BLOCK, (b + 1) * BLOCK)
+        e_ref = probs[b]
+        end_row = ends_ref[:, M + b * BLOCK : M + (b + 1) * BLOCK].astype(f32)
+        end_b = jnp.broadcast_to(end_row, (128, BLOCK)).T
+        weight = jnp.where(
+            (lane_q == 0) | (lane_q == 3), 1.0, jnp.where(lane_q == 7, -end_b, 0.0)
+        )
+
+        def bwd_pair(p, _):
+            lanes = pl.ds(pl.multiple_of(p * 128, 128), 128)
+            dol_pair = mixed[rows, lanes]
+            outs = []
+            for half in range(2):
+                head = 2 * p + half
+                keep = first_half if half == 0 else jnp.logical_not(first_half)
+                d_half = jnp.where(keep, dol_pair, jnp.zeros_like(dol_pair))
+                delta = delta_s[rows, :]
+                delta = jnp.where(lane_q // 4 == head, delta, jnp.zeros_like(delta))
+                d_full = jnp.concatenate([d_half, delta], axis=1)
+                e = e_ref[head, :, :]
+                ds = (dot_nt(d_full, value_full(lanes, keys)) * e.astype(f32)).astype(bf16)
+                dqx = dot_nn(ds, key_full(lanes, keys))
+                outs.append(dqx[:, 0:128])
+                hrows = pl.ds(pl.multiple_of(head * DH, DH), DH)
+                dkt[hrows, 0:keys] += dot_nn(qt[hrows, rows], ds)
+                dvt[hrows, 0:keys] += dot_nn(dolt[hrows, rows], e)
+                tail = jnp.sum(dqx[:, 128:256] * weight, axis=0, keepdims=True)
+                at = lax.broadcasted_iota(jnp.int32, (8, 128), 0) == head
+                small_ref[8:16, 0:128] += jnp.where(at, tail, 0.0)
+            dq = jnp.where(first_half, outs[0], outs[1]) * (1.0 / math.sqrt(DH))
+            q_s[rows, lanes] = dq.astype(bf16)
+            return 0
+
+        lax.fori_loop(0, HP, bwd_pair, 0)
+
+    gq_ref[...] = dot_nn(keyint[:, M:], q_s[...]).astype(bf16)
+
+    def rows_back(b, grads):
+        rows = pl.ds(pl.multiple_of(b * BLOCK, BLOCK), BLOCK)
+        dk = (dkt[:, rows] * LN2).astype(bf16).T
+        dv = dvt[:, rows].astype(bf16).T
+        k_s[rows, :] = dk
+        v_s[rows, :] = dv
+        return grads
+
+    lax.fori_loop(0, MB + NB, rows_back, 0)
+    gk_ref[...] = dot_nn(keyint[...], k_s[...]).astype(bf16)
+    gv_ref[...] = dot_nn(keyint[...], v_s[...]).astype(bf16)
+
+    def mem_back(b, sums):
+        rows = pl.ds(pl.multiple_of(b * BLOCK, BLOCK), BLOCK)
+        unit, _ = norm_stats(mem_ref[rows, :].astype(f32))
+        d_rows = dot_nt(k_s[rows, :], wk_ref[...]) + dot_nt(v_s[rows, :], wv_ref[...])
+        return sums[0] + col_sum8(d_rows * unit), sums[1] + col_sum8(d_rows)
+
+    def slot_back(b, sums):
+        rows = pl.ds(pl.multiple_of(b * BLOCK, BLOCK), BLOCK)
+        key_rows = pl.ds(pl.multiple_of(b * BLOCK + M, BLOCK), BLOCK)
+        unit, scale = norm_stats(x_ref[rows, :].astype(f32))
+        d_rows = dot_nt(k_s[key_rows, :], wk_ref[...]) + dot_nt(v_s[key_rows, :], wv_ref[...])
+        d_rows = d_rows + dot_nt(q_s[rows, :], wq_ref[...])
+        grad = norm_back(unit, scale, d_rows * gain1) + dres[rows, :]
+        ingrad_ref[rows, :] = grad.astype(bf16)
+        return sums[0] + col_sum8(d_rows * unit), sums[1] + col_sum8(d_rows)
+
+    sums = lax.fori_loop(0, MB, mem_back, (zero8, zero8))
+    gain1_sum, shift1_sum = lax.fori_loop(0, NB, slot_back, sums)
+    small_ref[0:1, :] = jnp.sum(gain1_sum, axis=0, keepdims=True)
+    small_ref[1:2, :] = jnp.sum(shift1_sum, axis=0, keepdims=True)
+    small_ref[2:3, :] = jnp.sum(gain2_sum, axis=0, keepdims=True)
+    small_ref[3:4, :] = jnp.sum(shift2_sum, axis=0, keepdims=True)
+
+
+def layer_call(counts, lengths, which, x, mem, ends, og, params):
+    S, D = x.shape
+    M = mem.shape[0]
+    R = M + S
+    gain1, shift1, wq, wk, wv, wo, slopes, gain2, shift2, w1, w2 = params
+    FF = w1.shape[1]
+    H = slopes.shape[0]
+    vmem = pl.BlockSpec(memory_space=pltpu.VMEM)
+    smem = pl.BlockSpec(memory_space=pltpu.SMEM)
+    V = pltpu.VMEM
+    scratch = [
+        V((D, R), bf16),
+        V((R, D), bf16),
+        V((R, D), bf16),
+        V((R, 128), bf16),
+        V((S, D), bf16),
+        V((D, S), bf16),
+        V((S, 128), f32),
+        V((S, D), f32),
+        V((S, D), bf16),
+        V((D, FF), f32),
+        V((D, FF), f32),
+        V((D, D), f32),
+        V((S, D), f32),
+        V((D, S), bf16),
+        V((S, 128), bf16),
+    ]
+    for b in range(S // BLOCK):
+        scratch.append(V((H, BLOCK, M + (b + 1) * BLOCK), bf16))
+    shapes = (
+        jax.ShapeDtypeStruct((S, D), bf16),
+        jax.ShapeDtypeStruct((S, D), bf16),
+        jax.ShapeDtypeStruct((D, D), bf16),
+        jax.ShapeDtypeStruct((D, D), bf16),
+        jax.ShapeDtypeStruct((D, D), bf16),
+        jax.ShapeDtypeStruct((D, D), bf16),
+        jax.ShapeDtypeStruct((D, FF), bf16),
+        jax.ShapeDtypeStruct((D, FF), bf16),
+        jax.ShapeDtypeStruct((16, D), f32),
+    )
+    return pl.pallas_call(
+        layer_kernel,
+        out_shape=shapes,
+        in_specs=[smem, smem, smem] + [vmem] * 10 + [smem] + [vmem] * 4,
+        out_specs=[vmem] * len(shapes),
+        scratch_shapes=scratch,
+        compiler_params=pltpu.CompilerParams(vmem_limit_bytes=64 * 1024 * 1024 - 65536),
+        name="layer",
+    )(
+        counts, lengths, which, x, mem, ends, og,
+        gain1.reshape(1, D), shift1.reshape(1, D), wq, wk, wv, wo, slopes,
+        gain2.reshape(1, D), shift2.reshape(1, D), w1, w2,
+    )
 
 
 def layer_norm(values, gain, shift):
@@ -28,7 +437,7 @@
     return (jnp.where(allowed[None], scores, -1e30), distance)
 
 
-def per_device(
+def spread_device(
     tokens,
     memory,
     segment_ends,
@@ -359,6 +768,54 @@
     )
 
 
+def whole_device(*args):
+    tokens, memory, segment_ends, memory_ends, counts, lengths = args[:6]
+    params = args[6:17]
+    output_grad = args[17]
+    D = tokens.shape[2]
+
+    def gather(array):
+        return lax.all_to_all(array, "blk", 0, 1, tiled=True)[0]
+
+    x = gather(tokens)
+    mem = gather(memory)
+    og = gather(output_grad)
+    ends = jnp.concatenate([gather(memory_ends), gather(segment_ends)])[None]
+    which = lax.axis_index("blk").astype(jnp.int32).reshape(1)
+    layer, in_grad, gq, gk, gv, go, gw1, gw2t, small = layer_call(
+        counts, lengths, which, x, mem, ends, og, params
+    )
+
+    def scatter(array):
+        return lax.all_to_all(array[None], "blk", 1, 0, tiled=True)
+
+    gq, gk, gv, go, gw1, gw2t, small = lax.psum(
+        (gq, gk, gv, go, gw1, gw2t, small), ("seq", "blk")
+    )
+    H = params[6].shape[0]
+    return (
+        scatter(layer),
+        scatter(in_grad),
+        small[0],
+        small[1],
+        gq.astype(f32),
+        gk.astype(f32),
+        gv.astype(f32),
+        go.astype(f32),
+        jnp.sum(small[8 : 8 + H], axis=1),
+        small[2],
+        small[3],
+        gw1.astype(f32),
+        gw2t.astype(f32).T,
+    )
+
+
+def per_device(*args):
+    if args[0].shape[0] == lax.axis_size("blk"):
+        return whole_device(*args)
+    return spread_device(*args)
+
+
 def solution(mesh):
     placed = (
         P("seq", "blk", None),

time: 944 us -> 341 us (0.36)
  matrix products: 271 us -> 0 us
  waiting for transfers between devices: 319 us -> 84.9 us
  local copies, waits for them, and re-layouts: 199 us -> 23.2 us
  Pallas kernels: 0 us -> 90.6 us
  other arithmetic: 75.8 us -> 24.8 us
  blocking collectives: 46.3 us -> 79.2 us
  starting transfers between devices: 0.12 us -> 16.9 us
  loops' own time: 11.6 us -> 0 us
    dot_general x49 -> x0, matrix products: 271 us -> none  [the longest x14 58.7 us: block_scores(): jnp.einsum('qhd,khd->hqk', q_heads, key_block, preferred_element_type=jnp...]
    psum x1, waiting for transfers between devices: 183 us -> 69.8 us  [whole_device(): lax.psum((gq, gk, gv, go, gw1, gw2t, small), ('seq', 'blk'))]
    pallas_call x0 -> x1, Pallas kernels: none -> 90.6 us  [layer_call(): pl.pallas_call(layer_kernel, out_shape=shapes, in_specs=[smem, smem, smem...]
    all_gather x1 -> x0, waiting for transfers between devices: 73.6 us -> none  [per_device(): lax.all_gather(key_value, 'blk', axis=0, tiled=True)]
    reduce_scatter x1 -> x0, waiting for transfers between devices: 61.7 us -> none  [per_device(): lax.psum_scatter(pieces.reshape(lax.axis_size('blk') * key_rows, seq_coun...]
    dynamic_slice x38 -> x0, local copies, waits for them, and re-layouts: 55 us -> none  [the longest x20 23.6 us: attend(): lax.scan(stats_step, (start_max, jnp.zeros_like(start_max)), (key_heads,...]
    reshape x8 -> x0, local copies, waits for them, and re-layouts: 34.8 us -> none  [the longest x4 19.6 us: pick(): pair_rows[:, model_width:].reshape(-1, key_rows, head_count, head_dim)]
    all_to_all x0 -> x3, blocking collectives: none -> 32.1 us  [gather(): return lax.all_to_all(array, 'blk', 0, 1, tiled=True)[0]]
  transfers between devices with their start and end apart: 3 -> 5, of which waited for: 3 -> 4; matrix products, arithmetic and copies ran while one was open for 3% -> 9% of each run, Pallas kernels for 0% -> 0%
where the time goes in v1:
time: 341 us; the launch traced here: 334 us
  Pallas kernels  90.6 us (27%)
  waiting for transfers between devices  84.9 us (25%)
  blocking collectives  79.2 us (23%)
  other arithmetic  24.8 us (7%)
  local copies, waits for them, and re-layouts  23.2 us (7%)
  starting transfers between devices  16.9 us (5%)
  between operations  14.6 us (4%)
    pallas_call x1, Pallas kernels, layer_call(): pl.pallas_call(layer_kernel, out_shape=shapes, in_specs=[smem, smem, smem...  90.6 us
    psum x1, waiting for transfers between devices, whole_device(): lax.psum((gq, gk, gv, go, gw1, gw2t, small), ('seq', 'blk'))  69.8 us
    psum x1, blocking collectives, whole_device(): lax.psum((gq, gk, gv, go, gw1, gw2t, small), ('seq', 'blk'))  47.2 us
    all_to_all x3, blocking collectives, gather(): return lax.all_to_all(array, 'blk', 0, 1, tiled=True)[0]  32.1 us
    unnamed x18, local copies, waits for them, and re-layouts  15.6 us
    unnamed x2, other arithmetic  15.1 us
    all_to_all x2, waiting for transfers between devices, gather(): return lax.all_to_all(array, 'blk', 0, 1, tiled=True)[0]  12.2 us
    all_to_all x2, starting transfers between devices, gather(): return lax.all_to_all(array, 'blk', 0, 1, tiled=True)[0]  8.61 us
  transfers between devices with their start and end apart: 5, of which 4 were waited for; matrix products, arithmetic and copies ran while one was open for 9% of the time, Pallas kernels for 0%

profile of v1, /device:TPU:0, one launch (start us, length us, event | category | flops | bytes accessed | tf_op | source)
XLA Modules:
  0.0 334.3 jit_solution(12339657918708949468)
XLA Ops:
  7.2 1.3 all_to_all.26
  8.4 4.2 %all-to-all-start.2 = ((s32[2,1,256]{2,1,0:T(1,128)}), s32[2,1,256]{2,1,0:T(1,128)S(1)}, u32[]{:S(2)}, u32[]{:S(2)}) async-start(s32[2,1,256]{2,1,0:T(1,128)} %all_to_all.26), calls=%async_computation.2 | async-start | bytes 4096 | tf_op jit(solution)/shard_map/all_to_all | solution.py:778
  12.6 0.7 all_to_all.28
  13.3 3.1 all-to-all-done.2
  16.4 6.1 %all_to_all.77 = s32[2,1,512]{2,1,0:T(1,128)S(1)} all-to-all(s32[2,1,512]{2,1,0:T(1,128)S(1)} %all_to_all.28), channel_id=1, replica_groups=mesh['seq'=16,'blk'=2] {'blk'}, dimensions={0} | all-to-all | bytes 8192 | tf_op jit(solution)/shard_map/all_to_all | solution.py:778
  22.5 10.9 %all_to_all.78 = bf16[2,256,512]{2,1,0:T(8,128)(2,1)} all-to-all(bf16[2,256,512]{2,1,0:T(8,128)(2,1)} %param.19), channel_id=1, replica_groups=mesh['seq'=16,'blk'=2] {'blk'}, dimensions={0} | all-to-all | bytes 1048576 | tf_op jit(solution)/shard_map/all_to_all | solution.py:778
  33.4 15.1 %all_to_all.79 = bf16[2,512,512]{2,1,0:T(8,128)(2,1)} all-to-all(bf16[2,512,512]{2,1,0:T(8,128)(2,1)} %param.18), channel_id=1, replica_groups=mesh['seq'=16,'blk'=2] {'blk'}, dimensions={0} | all-to-all | bytes 2097152 | tf_op jit(solution)/shard_map/all_to_all | solution.py:778
  48.5 4.4 %all-to-all-start.4 = ((bf16[2,512,512]{2,1,0:T(8,128)(2,1)}), bf16[2,512,512]{2,1,0:T(8,128)(2,1)}, u32[]{:S(2)}, u32[]{:S(2)}) async-start(bf16[2,512,512]{2,1,0:T(8,128)(2,1)} %param.35), calls=%async_computation.4 | async-start | bytes 2097152 | tf_op jit(solution)/shard_map/all_to_all | solution.py:778
  53.6 9.1 %all-to-all-done.4 = bf16[2,512,512]{2,1,0:T(8,128)(2,1)} async-done(((bf16[2,512,512]{2,1,0:T(8,128)(2,1)}), bf16[2,512,512]{2,1,0:T(8,128)(2,1)}, u32[]{:S(2)}, u32[]{:S(2)}) %all-to-all-start.4) | async-done | bytes 1048608 | tf_op jit(solution)/shard_map/all_to_all | solution.py:778
  62.7 90.6 %layer.1 = (bf16[1024,512]{1,0:T(8,128)(2,1)}, bf16[1024,512]{1,0:T(8,128)(2,1)}, bf16[512,512]{1,0:T(8,128)(2,1)}, bf16[512,512]{1,0:T(8,128)(2,1)}, bf16[512,5...) custom-call(s32[2]{0:T(128)} %counts_ref.1, ...), custom_call_target="tpu_custom_call" | custom-call | tf_op jit(solution)/shard_map/layer/pallas_call | solution.py:406
  153.3 1.2 copy-done.1
  154.5 1.6 copy.42
  156.6 7.0 %reduce.1 = bf16[1024,512]{1,0:T(8,128)(2,1)S(1)} reduce(bf16[1024,1,512]{2,1,0:T(2,128)(2,1)S(1)} %bitcast.29, bf16[]{:T(256)} %broadcast), dimensions={1}, to_apply=%bitcast.25.reduce_sub_computation | reduce | bytes 2097154
  163.7 1.6 reshape.80
  165.2 3.8 %all-to-all-start.6 = ((bf16[2,2,131072]{2,1,0:T(2,128)(2,1)}), bf16[2,2,131072]{2,1,0:T(2,128)(2,1)S(1)}, u32[]{:S(2)}, u32[]{:S(2)}) async-start(bf16[2,2,131072]{2,1,0:T(2,128)(2,1)} %reshape.80), calls=%async_computation.6 | async-start | bytes 2097152 | tf_op jit(solution)/shard_map/all_to_all | solution.py:790
  169.1 2.8 copy.43
  171.9 8.0 %reduce = bf16[1024,512]{1,0:T(8,128)(2,1)} reduce(bf16[1024,1,512]{2,1,0:T(2,128)(2,1)S(1)} %bitcast.30, bf16[]{:T(256)} %broadcast), dimensions={1}, to_apply=%bitcast.26.reduce_sub_computation | reduce | bytes 2097154
  179.9 2.6 reshape.78
  182.6 2.9 all-to-all-done.6
  185.5 4.5 %all-to-all-start.5 = ((bf16[2,2,131072]{2,1,0:T(2,128)(2,1)}), bf16[2,2,131072]{2,1,0:T(2,128)(2,1)}, u32[]{:S(2)}, u32[]{:S(2)}) async-start(bf16[2,2,131072]{2,1,0:T(2,128)(2,1)} %reshape.78), calls=%async_computation.5 | async-start | bytes 2097152 | tf_op jit(solution)/shard_map/all_to_all | solution.py:790
  190.0 47.2 %psum.49 = f32[16,512]{1,0:T(8,128)S(1)} all-reduce(f32[16,512]{1,0:T(8,128)S(1)} %copy-done.4), channel_id=1, replica_groups=mesh['seq'=16,'blk'=2] {'seq','blk'}, use_global_device_ids=true, to_apply=%region_0.0 | all-reduce | flops 8192 | bytes 65536 | tf_op jit(solution)/shard_map/psum | solution.py:792
  238.4 0.9 reshape.81
  239.3 1.3 copy.39
  240.6 2.0 reshape.79
  242.5 1.3 copy.38
  243.8 69.8 %all-reduce.3.cloned.1.call-done = (bf16[2048,512]{0,1:T(8,128)(2,1)}, bf16[512,512]{1,0:T(8,128)(2,1)}, bf16[512,512]{1,0:T(8,128)(2,1)}, bf16[512,512]{1,0:T(8...) async-done(((bf16[2048,512]{0,1:T(8,128)(2,1)}, bf16[512,512]{1,0:T(8,128)(2,1)}, bf16[512,512]{1,0:T(8,128)(2,1)}, bf16[512,512]{1,0:T(8,128)(2,1)}, ...) | async-done | bytes 6291472 | tf_op jit(solution)/shard_map/psum | solution.py:792
  313.6 2.2 convert_element_type.16
  315.8 2.1 convert_element_type.17
  317.9 1.1 convert_element_type.18
  319.0 1.1 convert_element_type.19
  320.1 4.3 %copy.37 = f32[2048,512]{1,0:T(8,128)} copy(bf16[2048,512]{0,1:T(8,128)(2,1)} %get-tuple-element.70) | data formatting | bytes 6291456
  324.4 2.5 convert_element_type.20
  (17 shorter events, 2.4 us)
Async XLA Ops:
  8.4 8.0 %all-to-all-start.2 = ((s32[2,1,256]{2,1,0:T(1,128)}), s32[2,1,256]{2,1,0:T(1,128)S(1)}, u32[]{:S(2)}, u32[]{:S(2)}) async-start(s32[2,1,256]{2,1,0:T(1,128)} %all_to_all.26), calls=%async_computation.2 | async-start | bytes 4096 | tf_op jit(solution)/shard_map/all_to_all | solution.py:778
  48.5 14.2 %all-to-all-start.4 = ((bf16[2,512,512]{2,1,0:T(8,128)(2,1)}), bf16[2,512,512]{2,1,0:T(8,128)(2,1)}, u32[]{:S(2)}, u32[]{:S(2)}) async-start(bf16[2,512,512]{2,1,0:T(8,128)(2,1)} %param.35), calls=%async_computation.4 | async-start | bytes 2097152 | tf_op jit(solution)/shard_map/all_to_all | solution.py:778
  52.9 260.7 %all-reduce.3.cloned.1.call-start = ((), (), s32[]{:S(2)}) async-start(), calls=%async_computation.7 | async-start | bytes 12582912 | tf_op jit(solution)/shard_map/psum | solution.py:792
  153.2 1.2 copy-start.1
  165.2 20.3 %all-to-all-start.6 = ((bf16[2,2,131072]{2,1,0:T(2,128)(2,1)}), bf16[2,2,131072]{2,1,0:T(2,128)(2,1)S(1)}, u32[]{:S(2)}, u32[]{:S(2)}) async-start(bf16[2,2,131072]{2,1,0:T(2,128)(2,1)} %reshape.80), calls=%async_computation.6 | async-start | bytes 2097152 | tf_op jit(solution)/shard_map/all_to_all | solution.py:790
  179.9 10.0 %copy-start.4 = (f32[16,512]{1,0:T(8,128)S(1)}, f32[16,512]{1,0:T(8,128)}, u32[]{:S(2)}) copy-start(f32[16,512]{1,0:T(8,128)} %get-tuple-element.24) | copy-start | bytes 98308
  185.5 55.0 %all-to-all-start.5 = ((bf16[2,2,131072]{2,1,0:T(2,128)(2,1)}), bf16[2,2,131072]{2,1,0:T(2,128)(2,1)}, u32[]{:S(2)}, u32[]{:S(2)}) async-start(bf16[2,2,131072]{2,1,0:T(2,128)(2,1)} %reshape.78), calls=%async_computation.5 | async-start | bytes 2097152 | tf_op jit(solution)/shard_map/all_to_all | solution.py:790
  313.6 4.4 %copy-start.3 = (bf16[512,512]{1,0:T(8,128)(2,1)S(1)}, bf16[512,512]{1,0:T(8,128)(2,1)}, u32[]{:S(2)}) copy-start(bf16[512,512]{1,0:T(8,128)(2,1)} %get-tuple-element.73) | copy-start | bytes 1572868
  313.6 5.5 %copy-start.2 = (bf16[512,512]{1,0:T(8,128)(2,1)S(1)}, bf16[512,512]{1,0:T(8,128)(2,1)}, u32[]{:S(2)}) copy-start(bf16[512,512]{1,0:T(8,128)(2,1)} %get-tuple-element.74) | copy-start | bytes 1572868
  320.1 4.3 %copy-start = (bf16[512,2048]{1,0:T(8,128)(2,1)S(1)}, bf16[512,2048]{1,0:T(8,128)(2,1)}, u32[]{:S(2)}) copy-start(bf16[512,2048]{1,0:T(8,128)(2,1)} %get-tuple-element.75) | copy-start | bytes 6291460
Sparse Core Ops, SparseCore 0:
  153.4 160.1 all-reduce.2

commit v2 on v1

--- a/solution.py
+++ b/solution.py
@@ -67,34 +67,43 @@
     return jnp.sum(value.reshape(-1, 8, value.shape[-1]), axis=0)
 
 
+def flip(bit):
+    return 1 - bit
+
+
 def layer_kernel(
+    talk,
     counts_ref,
     lengths_ref,
-    which_ref,
+    slopes_ref,
+    tokens_ref,
+    memory_ref,
+    ends_ref,
+    grad_ref,
+    gain1_ref,
+    shift1_ref,
+    gain2_ref,
+    shift2_ref,
+    wq_hbm,
+    wk_hbm,
+    wv_hbm,
+    wo_hbm,
+    w1_hbm,
+    w2_hbm,
+    layer_hbm,
+    ingrad_hbm,
+    grads_hbm,
+    small_ref,
     x_ref,
     mem_ref,
-    ends_ref,
     og_ref,
-    gain1_ref,
-    shift1_ref,
+    ends_s,
     wq_ref,
     wk_ref,
     wv_ref,
     wo_ref,
-    slopes_ref,
-    gain2_ref,
-    shift2_ref,
     w1_ref,
     w2_ref,
-    layer_ref,
-    ingrad_ref,
-    gq_ref,
-    gk_ref,
-    gv_ref,
-    go_ref,
-    gw1_ref,
-    gw2t_ref,
-    small_ref,
     keyint,
     k_s,
     v_s,
@@ -104,12 +113,30 @@
     rl_s,
     o_s,
     mixed,
-    gw1_s,
-    gw2t_s,
-    go_s,
+    second_s,
+    secondt,
+    ogt,
+    act_s,
+    dpre_s,
+    acc_s,
     dres,
     dolt,
     delta_s,
+    stage,
+    g_s,
+    rc_s,
+    r1_s,
+    r2_s,
+    sm_own,
+    sm_in,
+    load_sem,
+    ex_send,
+    ex_recv,
+    ar_send,
+    ar_recv,
+    sm_send,
+    sm_recv,
+    out_sem,
     *probs,
 ):
     S, D = x_ref.shape
@@ -121,19 +148,261 @@
     HP = H // 2
     NB = S // BLOCK
     MB = M // BLOCK
-    which = which_ref[0]
-    count = counts_ref[which]
-    length = lengths_ref[which]
+    SH = S // 2
+    MH = M // 2
+    KC = 512
+    CH = 512
+    NC = FF // CH
+
+    if talk:
+        seq = lax.axis_index("seq")
+        blk = lax.axis_index("blk")
+    else:
+        seq = 0
+        blk = 0
+    core = seq % 2
+    why = (seq // 2) % 2
+    zed = seq // 4
+
+    def at(z=None, y=None, c=None, x=None):
+        z = zed if z is None else z
+        y = why if y is None else y
+        c = core if c is None else c
+        return {"seq": z * 4 + y * 2 + c, "blk": blk if x is None else x}
+
+    sibling = at(c=flip(core))
+    partner = at(x=flip(blk))
+    z_to = [zed + 1 - 2 * (zed % 2), (zed + 2) % 4, 3 - zed]
+    z_peers = [(at(z=z), z) for z in z_to]
+    plane = blk * 2 + why
+    xy_peers = [
+        (at(y=flip(why)), blk * 2 + flip(why)),
+        (at(x=flip(blk)), flip(blk) * 2 + why),
+        (at(x=flip(blk), y=flip(why)), flip(blk) * 2 + flip(why)),
+    ]
+    z_group = (zed, z_peers)
+    xy_group = (plane, xy_peers)
+
+    def remote(src, dst, send, recv, device):
+        return pltpu.make_async_remote_copy(
+            src_ref=src,
+            dst_ref=dst,
+            send_sem=send,
+            recv_sem=recv,
+            device_id=device,
+            device_id_type=pl.DeviceIdType.MESH,
+        )
+
+    other = 1 - blk
+
+    def half_rows(half, size):
+        return pl.ds(pl.multiple_of(half * size, BLOCK), size)
+
+    def slot_piece(part, index, half, i):
+        src = tokens_ref if part == 0 else grad_ref
+        dst = x_ref if part == 0 else og_ref
+        rows = pl.ds(pl.multiple_of(half * SH + i * BLOCK, BLOCK), BLOCK)
+        return src.at[index, i * BLOCK : (i + 1) * BLOCK, :], dst.at[rows, :]
+
+    nslot = SH // BLOCK
+    loads = [
+        (memory_ref.at[blk], mem_ref.at[half_rows(blk, MH), :]),
+        (ends_ref.at[blk], ends_s.at[blk]),
+        (wk_hbm, wk_ref),
+        (wv_hbm, wv_ref),
+        (wq_hbm, wq_ref),
+    ]
+    loads += [slot_piece(0, blk, blk, i) for i in range(nslot)]
+    n_first = len(loads)
+    loads += [(wo_hbm, wo_ref), (w1_hbm, w1_ref), (w2_hbm, w2_ref)]
+    loads += [slot_piece(1, blk, blk, i) for i in range(nslot)]
+    copies = [
+        pltpu.make_async_copy(src, dst, load_sem.at[i]) for i, (src, dst) in enumerate(loads)
+    ]
+    sends = [
+        (memory_ref.at[other], mem_ref.at[half_rows(blk, MH), :]),
+        (ends_ref.at[other], ends_s.at[blk]),
+    ]
+    sends += [slot_piece(0, other, blk, i) for i in range(nslot)]
+    sends += [slot_piece(1, other, blk, i) for i in range(nslot)]
+    if talk:
+        exchange = [
+            remote(src, dst, ex_send.at[i], ex_recv.at[i], partner)
+            for i, (src, dst) in enumerate(sends)
+        ]
+    else:
+        local = [
+            (memory_ref.at[other], mem_ref.at[half_rows(other, MH), :]),
+            (ends_ref.at[other], ends_s.at[other]),
+        ]
+        local += [slot_piece(0, other, other, i) for i in range(nslot)]
+        local += [slot_piece(1, other, other, i) for i in range(nslot)]
+        exchange = [
+            pltpu.make_async_copy(src, dst, ex_send.at[i]) for i, (src, dst) in enumerate(local)
+        ]
+    for copy in copies[:n_first]:
+        copy.start()
+    if talk:
+        barrier = pltpu.get_barrier_semaphore()
+        greet = [sibling] + [d for d, _ in z_peers] + [d for d, _ in xy_peers]
+        for device in greet:
+            pl.semaphore_signal(
+                barrier, inc=1, device_id=device, device_id_type=pl.DeviceIdType.MESH
+            )
+        pl.semaphore_wait(barrier, len(greet))
+    for copy in exchange:
+        copy.start()
+    for copy in copies[n_first:]:
+        copy.start()
+
+    def arrive(i):
+        if talk:
+            exchange[i].wait_recv()
+        else:
+            exchange[i].wait()
+
+    units = []
+    for c in range(NC):
+        units.append((c * 2 * CH, 2 * CH, c % 3 == 2))
+    units.append((2 * FF, D, False))
+    for p in range(HP):
+        units.append((2 * FF + D + p * 384, 384, False))
+    half0 = core * (D // 2)
+    N1, N2 = D // 8, D // 32
+
+    def rows_at(start, size):
+        return pl.ds(pl.multiple_of(start, 16), size)
+
+    def unit_copies(u, phase):
+        col, width, z_first = units[u]
+        (g, peers1), (h, peers2) = (z_group, xy_group) if z_first else (xy_group, z_group)
+        cols = slice(col, col + width)
+        out = []
+        if phase == 0:
+            rows = rows_at((1 - core) * (D // 2), D // 2)
+            out.append((g_s.at[rows, cols], rc_s.at[:, cols], 0, sibling))
+        elif phase == 1:
+            for d, (device, index) in enumerate(peers1):
+                rows = rows_at(half0 + index * N1, N1)
+                out.append((g_s.at[rows, cols], r1_s.at[d, :, cols], 1 + d, device))
+        elif phase == 2:
+            for d, (device, index) in enumerate(peers2):
+                rows = rows_at(half0 + g * N1 + index * N2, N2)
+                out.append((g_s.at[rows, cols], r2_s.at[d, :, cols], 4 + d, device))
+        elif phase == 3:
+            rows = rows_at(half0 + g * N1 + h * N2, N2)
+            for d, (device, _) in enumerate(peers2):
+                out.append((g_s.at[rows, cols], grads_hbm.at[rows, cols], 7 + d, device))
+        elif phase == 4:
+            rows = rows_at(half0 + g * N1, N1)
+            for d, (device, _) in enumerate(peers1):
+                out.append((grads_hbm.at[rows, cols], grads_hbm.at[rows, cols], 10 + d, device))
+        else:
+            rows = rows_at(half0, D // 2)
+            out.append((grads_hbm.at[rows, cols], grads_hbm.at[rows, cols], 13, sibling))
+        return [
+            remote(src, dst, ar_send.at[u, k], ar_recv.at[u, k], device)
+            for src, dst, k, device in out
+        ]
+
+    def unit_add(u, phase):
+        col, width, z_first = units[u]
+        (g, _), (h, _) = (z_group, xy_group) if z_first else (xy_group, z_group)
+        cols = slice(col, col + width)
+        if phase == 0:
+            step = 64
+
+            def add(i, _):
+                rows = rows_at(half0 + i * step, step)
+                mine = g_s[rows, cols].astype(f32)
+                theirs = rc_s[rows_at(i * step, step), cols].astype(f32)
+                g_s[rows, cols] = (mine + theirs).astype(bf16)
+                return 0
+
+            lax.fori_loop(0, D // 2 // step, add, 0)
+        elif phase == 1:
+            rows = rows_at(half0 + g * N1, N1)
+            total = g_s[rows, cols].astype(f32)
+            for d in range(3):
+                total = total + r1_s[d, :, cols].astype(f32)
+            g_s[rows, cols] = total.astype(bf16)
+        elif phase == 2:
+            rows = rows_at(half0 + g * N1 + h * N2, N2)
+            total = g_s[rows, cols].astype(f32)
+            for d in range(3):
+                total = total + r2_s[d, :, cols].astype(f32)
+            g_s[rows, cols] = total.astype(bf16)
+
+    def unit_out(u):
+        col, width, z_first = units[u]
+        (g, _), (h, _) = (z_group, xy_group) if z_first else (xy_group, z_group)
+        cols = slice(col, col + width)
+        rows = rows_at(half0 + g * N1 + h * N2, N2) if talk else slice(0, D)
+        return pltpu.make_async_copy(g_s.at[rows, cols], grads_hbm.at[rows, cols], out_sem.at[u])
+
+    def advance(u, step):
+        if not talk:
+            return
+        if step > 0:
+            for copy in unit_copies(u, step - 1):
+                copy.wait()
+            unit_add(u, step - 1)
+        if step == 3:
+            unit_out(u).start()
+        if step == 4:
+            unit_out(u).wait()
+        if step < 6:
+            for copy in unit_copies(u, step):
+                copy.start()
+
     gain1 = gain1_ref[...]
     shift1 = shift1_ref[...]
     gain2 = gain2_ref[...]
     shift2 = shift2_ref[...]
+    count = counts_ref[blk]
+    length = lengths_ref[blk]
+
+    def project(normed, key_rows):
+        keyint[:, key_rows] = normed.T
+        k_s[key_rows, :] = dot_nn(normed, wk_ref[...]).astype(bf16)
+        v_s[key_rows, :] = dot_nn(normed, wv_ref[...]).astype(bf16)
+
+    def norm_mem(b):
+        rows = pl.ds(pl.multiple_of(b * BLOCK, BLOCK), BLOCK)
+        unit, _ = norm_stats(mem_ref[rows, :].astype(f32))
+        project((unit * gain1 + shift1).astype(bf16), rows)
+
+    def norm_slot(b):
+        rows = pl.ds(pl.multiple_of(b * BLOCK, BLOCK), BLOCK)
+        key_rows = pl.ds(pl.multiple_of(b * BLOCK + M, BLOCK), BLOCK)
+        unit, _ = norm_stats(x_ref[rows, :].astype(f32))
+        normed = (unit * gain1 + shift1).astype(bf16)
+        project(normed, key_rows)
+        query = (dot_nn(normed, wq_ref[...]) * (LOG2E / math.sqrt(DH))).astype(bf16)
+        q_s[rows, :] = query
+        qt[:, rows] = query.T
+
+    for copy in copies[:n_first]:
+        copy.wait()
+    mh = MH // BLOCK
+    lax.fori_loop(0, mh, lambda i, _: (norm_mem(blk * mh + i), 0)[1], 0)
+    lax.fori_loop(0, nslot, lambda i, _: (norm_slot(blk * nslot + i), 0)[1], 0)
+    arrive(0)
+    lax.fori_loop(0, mh, lambda i, _: (norm_mem(other * mh + i), 0)[1], 0)
+    arrive(1)
 
     lane = lax.broadcasted_iota(jnp.int32, (128, 128), 1)
     row = lax.broadcasted_iota(jnp.int32, (128, 128), 0)
+
+    def end_row(start, size):
+        if start < M:
+            half, off = start // MH, start % MH
+        else:
+            half, off = (start - M) // SH, MH + (start - M) % SH
+        return ends_s[half, :, off : off + size].astype(f32)
+
     for r in range(R // 128):
-        ends = ends_ref[:, r * 128 : (r + 1) * 128].astype(f32)
-        end_col = jnp.broadcast_to(ends, (128, 128)).T
+        end_col = jnp.broadcast_to(end_row(r * 128, 128), (128, 128)).T
         high = jnp.floor(end_col * (1.0 / 256.0)) * 256.0
         index = row + r * 128
         if r * 128 < M:
@@ -145,52 +414,37 @@
         extra = jnp.where(lane == 7, 1.0, jnp.where(lane > 7, 0.0, extra))
         kx[r * 128 : (r + 1) * 128, :] = extra.astype(bf16)
 
-    def project(normed, key_rows):
-        keyint[:, key_rows] = normed.T
-        k_s[key_rows, :] = dot_nn(normed, wk_ref[...]).astype(bf16)
-        v_s[key_rows, :] = dot_nn(normed, wv_ref[...]).astype(bf16)
-
-    def norm_mem(b, _):
-        rows = pl.ds(pl.multiple_of(b * BLOCK, BLOCK), BLOCK)
-        unit, _ = norm_stats(mem_ref[rows, :].astype(f32))
-        project((unit * gain1 + shift1).astype(bf16), rows)
-        return 0
-
-    def norm_slot(b, _):
-        rows = pl.ds(pl.multiple_of(b * BLOCK, BLOCK), BLOCK)
-        key_rows = pl.ds(pl.multiple_of(b * BLOCK + M, BLOCK), BLOCK)
-        unit, _ = norm_stats(x_ref[rows, :].astype(f32))
-        normed = (unit * gain1 + shift1).astype(bf16)
-        project(normed, key_rows)
-        query = (dot_nn(normed, wq_ref[...]) * (LOG2E / math.sqrt(DH))).astype(bf16)
-        q_s[rows, :] = query
-        qt[:, rows] = query.T
-        return 0
-
-    lax.fori_loop(0, MB, norm_mem, 0)
-    lax.fori_loop(0, NB, norm_slot, 0)
+    for i in range(nslot):
+        arrive(2 + i)
+        norm_slot(other * nslot + i)
 
     lane_q = lax.broadcasted_iota(jnp.int32, (BLOCK, 128), 1)
     first_half = lane_q < DH
     lane_row = lax.broadcasted_iota(jnp.int32, (1, 128), 1)
 
-    def key_full(lanes, keys):
-        return jnp.concatenate([k_s[0:keys, lanes], kx[0:keys, :]], axis=1)
-
-    def value_full(lanes, keys):
-        return jnp.concatenate([v_s[0:keys, lanes], jnp.ones((keys, 128), bf16)], axis=1)
+    def key_chunks(b):
+        end = M + (b + 1) * BLOCK
+        return [(start, min(KC, end - start)) for start in range(0, end, KC)]
+
+    def key_full(lanes, start, size):
+        return jnp.concatenate(
+            [k_s[start : start + size, lanes], kx[start : start + size, :]], axis=1
+        )
+
+    def value_full(lanes, start, size):
+        return jnp.concatenate(
+            [v_s[start : start + size, lanes], jnp.ones((size, 128), bf16)], axis=1
+        )
 
     def query_extra(head):
         slope = jnp.full((1, 128), slopes_ref[head] * LOG2E, f32)
         s1, s2, s3 = pieces_of(slope, 3)
-        at = jnp.where(lane_row >= 3, lane_row - 3, lane_row)
-        out = jnp.where(at == 0, s1, jnp.where(at == 1, s2, s3))
-        out = jnp.where(lane_row < 6, out, jnp.where(lane_row == 6, 1.0, 0.0))
-        return out
+        where = jnp.where(lane_row >= 3, lane_row - 3, lane_row)
+        out = jnp.where(where == 0, s1, jnp.where(where == 1, s2, s3))
+        return jnp.where(lane_row < 6, out, jnp.where(lane_row == 6, 1.0, 0.0))
 
     rl_s[...] = jnp.zeros_like(rl_s)
     for b in range(NB):
-        keys = M + (b + 1) * BLOCK
         rows = slice(b * BLOCK, (b + 1) * BLOCK)
         e_ref = probs[b]
 
@@ -203,17 +457,23 @@
                 q_half = jnp.where(keep, q_pair, jnp.zeros_like(q_pair))
                 extra = jnp.broadcast_to(query_extra(2 * p + half), (BLOCK, 128)).astype(bf16)
                 q_full = jnp.concatenate([q_half, extra], axis=1)
-                scores = dot_nt(q_full, key_full(lanes, keys))
-                diag = scores[:, keys - BLOCK :]
+                chunks = key_chunks(b)
+                scores = [dot_nt(q_full, key_full(lanes, k0, kn)) for k0, kn in chunks]
                 below = lax.broadcasted_iota(
                     jnp.int32, (BLOCK, BLOCK), 1
                 ) <= lax.broadcasted_iota(jnp.int32, (BLOCK, BLOCK), 0)
-                diag = jnp.where(below, diag, -1e30)
-                scores = jnp.concatenate([scores[:, : keys - BLOCK], diag], axis=1)
-                top = jnp.max(scores, axis=1, keepdims=True)
-                e = jnp.exp2(scores - top).astype(bf16)
-                e_ref[2 * p + half, :, :] = e
-                both = dot_nn(e, value_full(lanes, keys))
+                last = scores[-1]
+                cut = last.shape[1] - BLOCK
+                diag = jnp.where(below, last[:, cut:], -1e30)
+                scores[-1] = jnp.concatenate([last[:, :cut], diag], axis=1) if cut else diag
+                top = jnp.max(scores[0], axis=1, keepdims=True)
+                for part in scores[1:]:
+                    top = jnp.maximum(top, jnp.max(part, axis=1, keepdims=True))
+                both = jnp.zeros((BLOCK, 256), f32)
+                for part, (k0, kn) in zip(scores, chunks):
+                    e = jnp.exp2(part - top).astype(bf16)
+                    e_ref[2 * p + half, :, k0 : k0 + kn] = e
+                    both = both + dot_nn(e, value_full(lanes, k0, kn))
                 outs.append((both[:, 0:128], 1.0 / both[:, 128:256]))
             rl = jnp.where(first_half, outs[0][1], outs[1][1])
             o = jnp.where(first_half, outs[0][0], outs[1][0]) * rl
@@ -225,45 +485,68 @@
 
         lax.fori_loop(0, HP, fwd_pair, 0)
 
-    gw1_s[...] = jnp.zeros_like(gw1_s)
-    gw2t_s[...] = jnp.zeros_like(gw2t_s)
-    go_s[...] = jnp.zeros_like(go_s)
-    CH = 512
-
-    def feed(b, sums):
+    for copy in copies[n_first:]:
+        copy.wait()
+    for i in range(nslot):
+        arrive(2 + nslot + i)
+
+    def residual_of(rows):
+        return x_ref[rows, :].astype(f32) + dot_nn(mixed[rows, :], wo_ref[...])
+
+    def feed_prep(b, _):
         rows = pl.ds(pl.multiple_of(b * BLOCK, BLOCK), BLOCK)
-        mix = mixed[rows, :]
-        residual = x_ref[rows, :].astype(f32) + dot_nn(mix, wo_ref[...])
-        unit, scale = norm_stats(residual)
+        residual = residual_of(rows)
+        unit, _ = norm_stats(residual)
         second = (unit * gain2 + shift2).astype(bf16)
-        second_t = second.T
-        og = og_ref[rows, :]
-        og_t = og.T
-        out = residual
-        d_second = jnp.zeros((BLOCK, D), f32)
-        for c in range(FF // CH):
-            cols = slice(c * CH, (c + 1) * CH)
-            hidden = dot_nn(second, w1_ref[:, cols])
-            d_act = dot_nt(og, w2_ref[cols, :])
+        second_s[rows, :] = second
+        secondt[:, rows] = second.T
+        ogt[:, rows] = og_ref[rows, :].T
+        acc_s[rows, :] = residual
+        return 0
+
+    lax.fori_loop(0, NB, feed_prep, 0)
+    for c in range(NC):
+        cols = slice(c * CH, (c + 1) * CH)
+
+        def feed(b, _):
+            rows = pl.ds(pl.multiple_of(b * BLOCK, BLOCK), BLOCK)
+            hidden = dot_nn(second_s[rows, :], w1_ref[:, cols])
+            d_act = dot_nt(og_ref[rows, :], w2_ref[cols, :])
             act, slope = gelu_both(hidden)
             act = act.astype(bf16)
             d_pre = (d_act * slope).astype(bf16)
-            out = out + dot_nn(act, w2_ref[cols, :])
-            d_second = d_second + dot_nt(d_pre, w1_ref[:, cols])
-            gw2t_s[:, cols] += dot_nn(og_t, act)
-            gw1_s[:, cols] += dot_nn(second_t, d_pre)
-        layer_ref[rows, :] = out.astype(bf16)
-        d_residual = og.astype(f32) + norm_back(unit, scale, d_second * gain2)
+            act_s[rows, :] = act
+            dpre_s[rows, :] = d_pre
+            acc_s[rows, :] += dot_nn(act, w2_ref[cols, :])
+            d_second = dot_nt(d_pre, w1_ref[:, cols])
+            dres[rows, :] = d_second if c == 0 else dres[rows, :] + d_second
+            return 0
+
+        lax.fori_loop(0, NB, feed, 0)
+        base = c * 2 * CH
+        for r in range(D // BLOCK):
+            rows = slice(r * BLOCK, (r + 1) * BLOCK)
+            g_s[rows, base : base + CH] = dot_nn(secondt[rows, :], dpre_s[...]).astype(bf16)
+            g_s[rows, base + CH : base + 2 * CH] = dot_nn(ogt[rows, :], act_s[...]).astype(bf16)
+        ticks(advance, "feed", c)
+
+    def feed_post(b, sums):
+        rows = pl.ds(pl.multiple_of(b * BLOCK, BLOCK), BLOCK)
+        unit, scale = norm_stats(residual_of(rows))
+        stage[rows, :] = acc_s[rows, :].astype(bf16)
+        d_second = dres[rows, :]
+        d_residual = og_ref[rows, :].astype(f32) + norm_back(unit, scale, d_second * gain2)
         dres[rows, :] = d_residual
         d_branch = d_residual.astype(bf16)
-        go_s[...] += dot_nn(mix.T, d_branch)
+        act_s[rows, :] = d_branch
+        secondt[:, rows] = mixed[rows, :].T
         d_mixed = dot_nt(d_branch, wo_ref[...]).astype(bf16).astype(f32)
         rl_b = rl_s[rows, :]
         rl_wide = []
         for p in range(HP):
             first = jnp.broadcast_to(rl_b[:, 2 * p : 2 * p + 1], (BLOCK, 128))
-            other = jnp.broadcast_to(rl_b[:, 2 * p + 1 : 2 * p + 2], (BLOCK, 128))
-            rl_wide.append(jnp.where(first_half, first, other))
+            second = jnp.broadcast_to(rl_b[:, 2 * p + 1 : 2 * p + 2], (BLOCK, 128))
+            rl_wide.append(jnp.where(first_half, first, second))
         dol_b = (d_mixed * jnp.concatenate(rl_wide, axis=1)).astype(bf16)
         mixed[rows, :] = dol_b
         dolt[:, rows] = dol_b.T
@@ -273,33 +556,46 @@
             part = prod[:, (head // 2) * 128 : (head // 2 + 1) * 128]
             keep = first_half if head % 2 == 0 else jnp.logical_not(first_half)
             delta = jnp.sum(jnp.where(keep, part, 0.0), axis=1, keepdims=True)
-            for at, piece in enumerate(pieces_of(jnp.broadcast_to(-delta, (BLOCK, 128)), 3)):
-                packed = jnp.where(lane_q == 4 * head + at, piece, packed)
+            for k, piece in enumerate(pieces_of(jnp.broadcast_to(-delta, (BLOCK, 128)), 3)):
+                packed = jnp.where(lane_q == 4 * head + k, piece, packed)
         delta_s[rows, :] = packed.astype(bf16)
         return sums[0] + col_sum8(d_second * unit), sums[1] + col_sum8(d_second)
 
     zero8 = jnp.zeros((8, D), f32)
-    gain2_sum, shift2_sum = lax.fori_loop(0, NB, feed, (zero8, zero8))
-    gw1_ref[...] = gw1_s[...].astype(bf16)
-    gw2t_ref[...] = gw2t_s[...].astype(bf16)
-    go_ref[...] = go_s[...].astype(bf16)
-
-    dkt, dvt = gw1_s.at[:, 0:R], gw2t_s.at[:, 0:R]
-    dkt[...] = jnp.zeros((D, R), f32)
-    dvt[...] = jnp.zeros((D, R), f32)
+    gain2_sum, shift2_sum = lax.fori_loop(0, NB, feed_post, (zero8, zero8))
+    for r in range(D // BLOCK):
+        rows = slice(r * BLOCK, (r + 1) * BLOCK)
+        g_s[rows, 2 * FF : 2 * FF + D] = dot_nn(secondt[rows, :], act_s[...]).astype(bf16)
+
+    def give(result, hbm, k):
+        own = pltpu.make_async_copy(
+            result.at[half_rows(blk, SH), :], hbm.at[blk], load_sem.at[k]
+        )
+        theirs = result.at[half_rows(other, SH), :]
+        if talk:
+            away = remote(theirs, hbm.at[blk], ex_send.at[n_ex + k], ex_recv.at[n_ex + k], partner)
+        else:
+            away = pltpu.make_async_copy(theirs, hbm.at[other], ex_send.at[n_ex + k])
+        return own, away
+
+    n_ex = len(sends)
+    layer_copies = give(stage, layer_hbm, 0)
+    for copy in layer_copies:
+        copy.start()
+    ticks(advance, "post", 0)
+
     small_ref[...] = jnp.zeros_like(small_ref)
-    for b in range(NB):
-        keys = M + (b + 1) * BLOCK
-        rows = slice(b * BLOCK, (b + 1) * BLOCK)
-        e_ref = probs[b]
-        end_row = ends_ref[:, M + b * BLOCK : M + (b + 1) * BLOCK].astype(f32)
-        end_b = jnp.broadcast_to(end_row, (128, BLOCK)).T
-        weight = jnp.where(
-            (lane_q == 0) | (lane_q == 3), 1.0, jnp.where(lane_q == 7, -end_b, 0.0)
-        )
-
-        def bwd_pair(p, _):
-            lanes = pl.ds(pl.multiple_of(p * 128, 128), 128)
+    NK = R // KC
+    lane_w = (lane_q == 0) | (lane_q == 3)
+
+    def bwd_pair(p, slope_sums):
+        lanes = pl.ds(pl.multiple_of(p * 128, 128), 128)
+        acc_s[0 : 2 * NK * 128, :] = jnp.zeros((2 * NK * 128, KC), f32)
+        for b in range(NB):
+            rows = slice(b * BLOCK, (b + 1) * BLOCK)
+            e_ref = probs[b]
+            end_b = jnp.broadcast_to(end_row(M + b * BLOCK, BLOCK), (128, BLOCK)).T
+            weight = jnp.where(lane_w, 1.0, jnp.where(lane_q == 7, -end_b, 0.0))
             dol_pair = mixed[rows, lanes]
             outs = []
             for half in range(2):
@@ -309,71 +605,204 @@
                 delta = delta_s[rows, :]
                 delta = jnp.where(lane_q // 4 == head, delta, jnp.zeros_like(delta))
                 d_full = jnp.concatenate([d_half, delta], axis=1)
-                e = e_ref[head, :, :]
-                ds = (dot_nt(d_full, value_full(lanes, keys)) * e.astype(f32)).astype(bf16)
-                dqx = dot_nn(ds, key_full(lanes, keys))
+                hrows = pl.ds(pl.multiple_of(head * DH, DH), DH)
+                q_t = qt[hrows, rows]
+                d_t = dolt[hrows, rows]
+                dqx = jnp.zeros((BLOCK, 256), f32)
+                for j, (k0, kn) in enumerate(key_chunks(b)):
+                    e = e_ref[head, :, k0 : k0 + kn]
+                    ds = (dot_nt(d_full, value_full(lanes, k0, kn)) * e.astype(f32)).astype(bf16)
+                    dqx = dqx + dot_nn(ds, key_full(lanes, k0, kn))
+                    at_k = j * 128 + half * DH
+                    acc_s[at_k : at_k + DH, 0:kn] += dot_nn(q_t, ds)
+                    at_v = (NK + j) * 128 + half * DH
+                    acc_s[at_v : at_v + DH, 0:kn] += dot_nn(d_t, e)
                 outs.append(dqx[:, 0:128])
-                hrows = pl.ds(pl.multiple_of(head * DH, DH), DH)
-                dkt[hrows, 0:keys] += dot_nn(qt[hrows, rows], ds)
-                dvt[hrows, 0:keys] += dot_nn(dolt[hrows, rows], e)
                 tail = jnp.sum(dqx[:, 128:256] * weight, axis=0, keepdims=True)
-                at = lax.broadcasted_iota(jnp.int32, (8, 128), 0) == head
-                small_ref[8:16, 0:128] += jnp.where(at, tail, 0.0)
+                here = lax.broadcasted_iota(jnp.int32, (8, 128), 0) == head
+                slope_sums = slope_sums + jnp.where(here, tail, 0.0)
             dq = jnp.where(first_half, outs[0], outs[1]) * (1.0 / math.sqrt(DH))
             q_s[rows, lanes] = dq.astype(bf16)
-            return 0
-
-        lax.fori_loop(0, HP, bwd_pair, 0)
-
-    gq_ref[...] = dot_nn(keyint[:, M:], q_s[...]).astype(bf16)
-
-    def rows_back(b, grads):
-        rows = pl.ds(pl.multiple_of(b * BLOCK, BLOCK), BLOCK)
-        dk = (dkt[:, rows] * LN2).astype(bf16).T
-        dv = dvt[:, rows].astype(bf16).T
-        k_s[rows, :] = dk
-        v_s[rows, :] = dv
-        return grads
-
-    lax.fori_loop(0, MB + NB, rows_back, 0)
-    gk_ref[...] = dot_nn(keyint[...], k_s[...]).astype(bf16)
-    gv_ref[...] = dot_nn(keyint[...], v_s[...]).astype(bf16)
+            for k in range(HP):
+                if has_ticks("bwd", k * NB + b):
+
+                    @pl.when(p == k)
+                    def _():
+                        ticks(advance, "bwd", k * NB + b)
+
+        for j in range(NK):
+            dk = (acc_s[j * 128 : (j + 1) * 128, :] * LN2).astype(bf16).T
+            k_s[j * KC : (j + 1) * KC, lanes] = dk
+            dv = acc_s[(NK + j) * 128 : (NK + j + 1) * 128, :].astype(bf16).T
+            v_s[j * KC : (j + 1) * KC, lanes] = dv
+        for r in range(D // BLOCK):
+            rows = slice(r * BLOCK, (r + 1) * BLOCK)
+            gq = dot_nn(keyint[rows, M:], q_s[:, lanes]).astype(bf16)
+            pair = jnp.concatenate([k_s[:, lanes], v_s[:, lanes]], axis=1)
+            gkv = dot_nn(keyint[rows, :], pair).astype(bf16)
+            col = 2 * FF + D + p * 384
+            g_s[rows, pl.ds(pl.multiple_of(col, 128), 128)] = gq
+            g_s[rows, pl.ds(pl.multiple_of(col + 128, 128), 256)] = gkv
+        for k in range(HP):
+            if has_ticks("pair", k):
+
+                @pl.when(p == k)
+                def _():
+                    ticks(advance, "pair", k)
+
+        return slope_sums
+
+    slope_sums = lax.fori_loop(0, HP, bwd_pair, jnp.zeros((8, 128), f32))
+
+    def key_back(key_rows):
+        return dot_nt(k_s[key_rows, :], wk_ref[...]) + dot_nt(v_s[key_rows, :], wv_ref[...])
 
     def mem_back(b, sums):
         rows = pl.ds(pl.multiple_of(b * BLOCK, BLOCK), BLOCK)
         unit, _ = norm_stats(mem_ref[rows, :].astype(f32))
-        d_rows = dot_nt(k_s[rows, :], wk_ref[...]) + dot_nt(v_s[rows, :], wv_ref[...])
+        d_rows = key_back(rows)
         return sums[0] + col_sum8(d_rows * unit), sums[1] + col_sum8(d_rows)
 
     def slot_back(b, sums):
         rows = pl.ds(pl.multiple_of(b * BLOCK, BLOCK), BLOCK)
         key_rows = pl.ds(pl.multiple_of(b * BLOCK + M, BLOCK), BLOCK)
         unit, scale = norm_stats(x_ref[rows, :].astype(f32))
-        d_rows = dot_nt(k_s[key_rows, :], wk_ref[...]) + dot_nt(v_s[key_rows, :], wv_ref[...])
-        d_rows = d_rows + dot_nt(q_s[rows, :], wq_ref[...])
+        d_rows = key_back(key_rows) + dot_nt(q_s[rows, :], wq_ref[...])
         grad = norm_back(unit, scale, d_rows * gain1) + dres[rows, :]
-        ingrad_ref[rows, :] = grad.astype(bf16)
+        stage[rows, :] = grad.astype(bf16)
         return sums[0] + col_sum8(d_rows * unit), sums[1] + col_sum8(d_rows)
 
-    sums = lax.fori_loop(0, MB, mem_back, (zero8, zero8))
-    gain1_sum, shift1_sum = lax.fori_loop(0, NB, slot_back, sums)
-    small_ref[0:1, :] = jnp.sum(gain1_sum, axis=0, keepdims=True)
-    small_ref[1:2, :] = jnp.sum(shift1_sum, axis=0, keepdims=True)
-    small_ref[2:3, :] = jnp.sum(gain2_sum, axis=0, keepdims=True)
-    small_ref[3:4, :] = jnp.sum(shift2_sum, axis=0, keepdims=True)
-
-
-def layer_call(counts, lengths, which, x, mem, ends, og, params):
-    S, D = x.shape
-    M = mem.shape[0]
+    layer_copies[0].wait()
+    if talk:
+        layer_copies[1].wait_send()
+    else:
+        layer_copies[1].wait()
+    sums = (zero8, zero8)
+    ingrad_own, ingrad_away = give(stage, ingrad_hbm, 1)
+    for i in range(nslot):
+        sums = slot_back(other * nslot + i, sums)
+        ticks(advance, "tail", i)
+    ingrad_away.start()
+    sums = lax.fori_loop(0, MB, mem_back, sums)
+    ticks(advance, "tail", nslot)
+    for i in range(nslot):
+        sums = slot_back(blk * nslot + i, sums)
+        ticks(advance, "tail", nslot + 1 + i)
+    ingrad_own.start()
+    gain1_sum, shift1_sum = sums
+    sm_own[0] = jnp.zeros_like(sm_own[0])
+    for k, part in enumerate((gain1_sum, shift1_sum, gain2_sum, shift2_sum)):
+        sm_own[0, k : k + 1, :] = jnp.sum(part, axis=0, keepdims=True)
+    total = jnp.broadcast_to(jnp.sum(slope_sums, axis=1, keepdims=True), (8, 128))
+    sm_own[0, 4:5, 0:128] = jnp.sum(
+        jnp.where(lax.broadcasted_iota(jnp.int32, (8, 128), 0)
+                  == lax.broadcasted_iota(jnp.int32, (8, 128), 1), total, 0.0),
+        axis=0, keepdims=True)
+
+    if talk:
+        k = 0
+        for level, devices in enumerate(
+            ([sibling], [d for d, _ in z_peers], [d for d, _ in xy_peers])
+        ):
+            hops = []
+            for device in devices:
+                hops.append(
+                    remote(sm_own.at[level], sm_in.at[k], sm_send.at[k], sm_recv.at[k], device)
+                )
+                k += 1
+            for hop in hops:
+                hop.start()
+            ticks(advance, "small", level)
+            total = sm_own[level]
+            for i, hop in enumerate(hops):
+                hop.wait()
+                total = total + sm_in[k - len(hops) + i]
+            sm_own[level + 1] = total
+        small_ref[...] = sm_own[3]
+    else:
+        for level in range(3):
+            ticks(advance, "small", level)
+        small_ref[...] = sm_own[0]
+    ticks(advance, "last", 0)
+    ingrad_own.wait()
+    if not talk:
+        for u in range(len(units)):
+            unit_out(u).start()
+            unit_out(u).wait()
+    if talk:
+        for copy in exchange:
+            copy.wait_send()
+        layer_copies[1].wait_recv()
+    ingrad_away.wait()
+
+
+SCHEDULE = {}
+
+
+def plan(points):
+    for key, moves in points.items():
+        SCHEDULE[key] = moves
+
+
+def has_ticks(kind, index):
+    return (kind, index) in SCHEDULE
+
+
+def ticks(advance, kind, index):
+    for u, step in SCHEDULE.get((kind, index), ()):
+        advance(u, step)
+
+
+def make_plan():
+    points = [("feed", c) for c in range(4)] + [("post", 0)]
+    for k in range(4):
+        points += [("bwd", k * 4 + b) for b in range(4)] + [("pair", k)]
+    points += [("tail", i) for i in range(5)]
+    points += [("small", i) for i in range(3)] + [("last", 0)]
+    where = {key: i for i, key in enumerate(points)}
+    ready = [where["feed", c] for c in range(4)] + [where["post", 0]]
+    ready += [where["pair", k] for k in range(4)]
+    table = {}
+    for u, start in enumerate(ready):
+        spot = start
+        for step in range(7):
+            spot = min(spot, len(points) - 1)
+            table.setdefault(spot, []).append((u, step))
+            kind = points[spot][0]
+            spot += 1 if kind in ("feed", "post", "tail", "small", "pair") else 2
+    for spot, moves in table.items():
+        SCHEDULE[points[spot]] = tuple(sorted(moves, key=lambda move: (move[1], move[0])))
+
+
+make_plan()
+
+
+def layer_call(counts, lengths, tokens, memory, ends, grad, params, talk=True):
+    _, SH, D = tokens.shape
+    MH = memory.shape[1]
+    S, M = 2 * SH, 2 * MH
     R = M + S
     gain1, shift1, wq, wk, wv, wo, slopes, gain2, shift2, w1, w2 = params
     FF = w1.shape[1]
     H = slopes.shape[0]
     vmem = pl.BlockSpec(memory_space=pltpu.VMEM)
     smem = pl.BlockSpec(memory_space=pltpu.SMEM)
+    hbm = pl.BlockSpec(memory_space=pl.ANY)
     V = pltpu.VMEM
+    G = 2 * FF + 4 * D
+    units = FF // 512 + 1 + H // 2
+    dma = pltpu.SemaphoreType.DMA
     scratch = [
+        V((S, D), bf16),
+        V((M, D), bf16),
+        V((S, D), bf16),
+        V((2, 1, MH + SH), jnp.int32),
+        V((D, D), bf16),
+        V((D, D), bf16),
+        V((D, D), bf16),
+        V((D, D), bf16),
+        V((D, FF), bf16),
+        V((FF, D), bf16),
         V((D, R), bf16),
         V((R, D), bf16),
         V((R, D), bf16),
@@ -383,38 +812,54 @@
         V((S, 128), f32),
         V((S, D), f32),
         V((S, D), bf16),
-        V((D, FF), f32),
-        V((D, FF), f32),
-        V((D, D), f32),
+        V((S, D), bf16),
+        V((D, S), bf16),
+        V((D, S), bf16),
+        V((S, 512), bf16),
+        V((S, 512), bf16),
+        V((S, D), f32),
         V((S, D), f32),
         V((D, S), bf16),
         V((S, 128), bf16),
+        V((S, D), bf16),
+        V((D, G), bf16),
+        V((D // 2, G), bf16),
+        V((3, D // 8, G), bf16),
+        V((3, D // 32, G), bf16),
+        V((4, 8, D), f32),
+        V((7, 8, D), f32),
+        dma((16,)),
+        dma((10,)),
+        dma((10,)),
+        dma((units, 14)),
+        dma((units, 14)),
+        dma((7,)),
+        dma((7,)),
+        dma((units,)),
     ]
     for b in range(S // BLOCK):
         scratch.append(V((H, BLOCK, M + (b + 1) * BLOCK), bf16))
     shapes = (
-        jax.ShapeDtypeStruct((S, D), bf16),
-        jax.ShapeDtypeStruct((S, D), bf16),
-        jax.ShapeDtypeStruct((D, D), bf16),
-        jax.ShapeDtypeStruct((D, D), bf16),
-        jax.ShapeDtypeStruct((D, D), bf16),
-        jax.ShapeDtypeStruct((D, D), bf16),
-        jax.ShapeDtypeStruct((D, FF), bf16),
-        jax.ShapeDtypeStruct((D, FF), bf16),
-        jax.ShapeDtypeStruct((16, D), f32),
-    )
+        jax.ShapeDtypeStruct((2, SH, D), bf16),
+        jax.ShapeDtypeStruct((2, SH, D), bf16),
+        jax.ShapeDtypeStruct((D, G), bf16),
+        jax.ShapeDtypeStruct((8, D), f32),
+    )
+    extra = {"collective_id": 1, "has_side_effects": True} if talk else {}
     return pl.pallas_call(
-        layer_kernel,
+        functools.partial(layer_kernel, talk),
         out_shape=shapes,
-        in_specs=[smem, smem, smem] + [vmem] * 10 + [smem] + [vmem] * 4,
-        out_specs=[vmem] * len(shapes),
+        in_specs=[smem] * 3 + [hbm] * 4 + [vmem] * 4 + [hbm] * 6,
+        out_specs=[hbm, hbm, hbm, vmem],
         scratch_shapes=scratch,
-        compiler_params=pltpu.CompilerParams(vmem_limit_bytes=64 * 1024 * 1024 - 65536),
+        compiler_params=pltpu.CompilerParams(
+            vmem_limit_bytes=64 * 1024 * 1024 - 65536, **extra
+        ),
         name="layer",
     )(
-        counts, lengths, which, x, mem, ends, og,
-        gain1.reshape(1, D), shift1.reshape(1, D), wq, wk, wv, wo, slopes,
-        gain2.reshape(1, D), shift2.reshape(1, D), w1, w2,
+        counts, lengths, slopes, tokens, memory, ends, grad,
+        gain1.reshape(1, D), shift1.reshape(1, D), gain2.reshape(1, D), shift2.reshape(1, D),
+        wq, wk, wv, wo, w1, w2,
     )
 
 
@@ -768,50 +1213,98 @@
     )
 
 
+def widen_kernel(ga, gb, gc, layer_in, grad_in, small, *outs):
+    gw1, gw2, go, gq, gk, gv, layer, grad, gain1, shift1, slopes, gain2, shift2 = outs
+    half = ga.shape[1] // 2
+    gw1[...] = ga[:, :half].astype(f32)
+    gw2[...] = ga[:, half:].astype(f32).T
+    go[...] = gb[...].astype(f32)
+    for i, out in enumerate((gq, gk, gv)):
+        out[...] = gc[:, i * 128 : (i + 1) * 128].astype(f32)
+    layer[...] = layer_in[...]
+    grad[...] = grad_in[...]
+
+    @pl.when((pl.program_id(0) == 0) & (pl.program_id(1) == 0))
+    def _():
+        for i, out in enumerate((gain1, shift1, gain2, shift2)):
+            out[...] = small[i : i + 1, :]
+        slopes[...] = small[4:5, 0:128]
+
+
+def widen(grads, layer, in_grad, small, D, FF):
+    RB = D // 2
+    LB = layer.shape[0] // 8
+    out = [
+        ((D, FF), (RB, 512), lambda c, r: (r, c)),
+        ((FF, D), (512, RB), lambda c, r: (c, r)),
+        ((D, D), (RB, 128), lambda c, r: (r, c)),
+        ((D, D), (RB, 128), lambda c, r: (r, c)),
+        ((D, D), (RB, 128), lambda c, r: (r, c)),
+        ((D, D), (RB, 128), lambda c, r: (r, c)),
+        ((8 * LB, D), (LB, D), lambda c, r: (2 * c + r, 0)),
+        ((8 * LB, D), (LB, D), lambda c, r: (2 * c + r, 0)),
+    ]
+    kinds = [f32] * 6 + [bf16] * 2
+    shapes = [jax.ShapeDtypeStruct(shape, kind) for (shape, _, _), kind in zip(out, kinds)]
+    specs = [pl.BlockSpec(block, index) for _, block, index in out]
+    for width in (D, D, 128, D, D):
+        shapes.append(jax.ShapeDtypeStruct((1, width), f32))
+        specs.append(pl.BlockSpec((1, width), lambda c, r: (0, 0)))
+    go_at = 2 * FF // 128
+    head_at = (2 * FF + D) // 384
+    return pl.pallas_call(
+        widen_kernel,
+        grid=(4, 2),
+        out_shape=shapes,
+        in_specs=[
+            pl.BlockSpec((RB, 1024), lambda c, r: (r, c)),
+            pl.BlockSpec((RB, 128), lambda c, r: (r, go_at + c)),
+            pl.BlockSpec((RB, 384), lambda c, r: (r, head_at + c)),
+            pl.BlockSpec((LB, D), lambda c, r: (2 * c + r, 0)),
+            pl.BlockSpec((LB, D), lambda c, r: (2 * c + r, 0)),
+            pl.BlockSpec((8, D), lambda c, r: (0, 0)),
+        ],
+        out_specs=specs,
+        compiler_params=pltpu.CompilerParams(vmem_limit_bytes=32 * 1024 * 1024),
+        name="widen",
+    )(grads, grads, grads, layer, in_grad, small)
+
+
 def whole_device(*args):
     tokens, memory, segment_ends, memory_ends, counts, lengths = args[:6]
     params = args[6:17]
     output_grad = args[17]
     D = tokens.shape[2]
-
-    def gather(array):
-        return lax.all_to_all(array, "blk", 0, 1, tiled=True)[0]
-
-    x = gather(tokens)
-    mem = gather(memory)
-    og = gather(output_grad)
-    ends = jnp.concatenate([gather(memory_ends), gather(segment_ends)])[None]
-    which = lax.axis_index("blk").astype(jnp.int32).reshape(1)
-    layer, in_grad, gq, gk, gv, go, gw1, gw2t, small = layer_call(
-        counts, lengths, which, x, mem, ends, og, params
-    )
-
-    def scatter(array):
-        return lax.all_to_all(array[None], "blk", 1, 0, tiled=True)
-
-    gq, gk, gv, go, gw1, gw2t, small = lax.psum(
-        (gq, gk, gv, go, gw1, gw2t, small), ("seq", "blk")
-    )
+    FF = params[9].shape[1]
     H = params[6].shape[0]
+    ends = jnp.concatenate([memory_ends, segment_ends], axis=1)[:, None]
+    layer, in_grad, grads, small = layer_call(
+        counts, lengths, tokens, memory, ends, output_grad, params
+    )
+    gw1, gw2, go, gq, gk, gv, layer, in_grad, *rows = widen(
+        grads, layer.reshape(-1, D), in_grad.reshape(-1, D), small, D, FF
+    )
+    gain1, shift1, slopes, gain2, shift2 = (row[0] for row in rows)
     return (
-        scatter(layer),
-        scatter(in_grad),
-        small[0],
-        small[1],
-        gq.astype(f32),
-        gk.astype(f32),
-        gv.astype(f32),
-        go.astype(f32),
-        jnp.sum(small[8 : 8 + H], axis=1),
-        small[2],
-        small[3],
-        gw1.astype(f32),
-        gw2t.astype(f32).T,
+        layer.reshape(tokens.shape),
+        in_grad.reshape(tokens.shape),
+        gain1,
+        shift1,
+        gq,
+        gk,
+        gv,
+        go,
+        slopes[:H],
+        gain2,
+        shift2,
+        gw1,
+        gw2,
     )
 
 
 def per_device(*args):
-    if args[0].shape[0] == lax.axis_size("blk"):
+    whole = args[0].shape[0] == lax.axis_size("blk") == 2 and lax.axis_size("seq") == 16
+    if whole:
         return whole_device(*args)
     return spread_device(*args)
 

time: 341 us -> 214 us (0.63); the launches traced: 334 us -> 214 us
  Pallas kernels: 90.6 us -> 205 us
  waiting for transfers between devices: 84.9 us -> 0 us
  blocking collectives: 79.2 us -> 0 us
  other arithmetic: 24.8 us -> 0.7 us
  starting transfers between devices: 16.9 us -> 0 us
  local copies, waits for them, and re-layouts: 23.2 us -> 7.06 us
  between operations: 14.6 us -> 0.67 us
    pallas_call x1 -> x2, Pallas kernels: 90.6 us -> 205 us  [the longest x1 199 us: layer_call(): pl.pallas_call(functools.partial(layer_kernel, talk), out_shape=shapes, i...]
    psum x1 -> x0, waiting for transfers between devices: 69.8 us -> none  [whole_device(): lax.psum((gq, gk, gv, go, gw1, gw2t, small), ('seq', 'blk'))]
    psum x1 -> x0, blocking collectives: 47.2 us -> none  [whole_device(): lax.psum((gq, gk, gv, go, gw1, gw2t, small), ('seq', 'blk'))]
    all_to_all x3 -> x0, blocking collectives: 32.1 us -> none  [gather(): return lax.all_to_all(array, 'blk', 0, 1, tiled=True)[0]]
    all_to_all x4 -> x0, starting transfers between devices: 16.9 us -> none  [the longest x2 8.61 us: gather(): return lax.all_to_all(array, 'blk', 0, 1, tiled=True)[0]]
    all_to_all x4 -> x0, waiting for transfers between devices: 15.1 us -> none  [the longest x2 12.2 us: gather(): return lax.all_to_all(array, 'blk', 0, 1, tiled=True)[0]]
    unnamed x2 -> x0, other arithmetic: 15.1 us -> none
    unnamed x18 -> x8, local copies, waits for them, and re-layouts: 15.6 us -> 5.94 us
  transfers between devices with their start and end apart: 5 -> 0, of which waited for: 4 -> 0; matrix products, arithmetic and copies ran while one was open for 9% -> 0% of each run, Pallas kernels for 0% -> 0%
where the time goes in v2:
time: 214 us
  Pallas kernels  205 us (96%)
  local copies, waits for them, and re-layouts  7.06 us (3%)
    pallas_call x1, Pallas kernels, layer_call(): pl.pallas_call(functools.partial(layer_kernel, talk), out_shape=shapes, i...  199 us
    pallas_call x1, Pallas kernels, widen(): pl.pallas_call(widen_kernel, grid=(4, 2), out_shape=shapes, in_specs=[pl....  6.55 us
    unnamed x8, local copies, waits for them, and re-layouts  5.94 us

profile of v2, /device:TPU:0, one launch (start us, length us, event | category | flops | bytes accessed | tf_op | source)
XLA Modules:
  0.0 213.7 jit_solution(2433576449397939805)
XLA Ops:
  0.6 0.7 pad_add_fusion
  1.3 0.6 broadcast_in_dim.3.ends_ref
  1.9 198.7 %layer.1 = (bf16[2,512,512]{2,1,0:T(8,128)(2,1)}, bf16[2,512,512]{2,1,0:T(8,128)(2,1)}, bf16[512,6144]{1,0:T(8,128)(2,1)}, f32[8,512]{1,0:T(8,128)}) custom-call(s32[2]{0:T(128)} %counts_ref.1, s32[2]{0:T(128)} %lengths_ref.1, f32[8]{0:T(128)} %slopes_ref.1, bf16[2,512,512]{2,1,0:T(8,128)(2,1)} %tokens_ref.1, bf16[2,256,512]{2,1,0:T(8,128)(2,1)} %memory_ref.1, ...), custom_call_target="tpu_custom_call" | custom-call | tf_op jit(solution)/shard_map/layer/pallas_call | solution.py:849
  200.7 0.0 copy-start
  200.7 2.8 %copy-done = bf16[512,6144]{1,0:T(8,128)(2,1)S(1)} copy-done((bf16[512,6144]{1,0:T(8,128)(2,1)S(1)}, bf16[512,6144]{1,0:T(8,128)(2,1)}, u32[]{:S(2)}) %copy-start) | copy-done | bytes 6291480
  203.5 0.0 copy-start.1
  203.5 1.2 copy-done.1
  204.7 0.0 copy-start.2
  204.7 1.2 copy-done.2
  205.9 0.0 copy-start.3
  205.9 0.7 copy-done.3
  206.6 6.6 %widen.1 = (f32[512,2048]{1,0:T(8,128)}, f32[2048,512]{1,0:T(8,128)}, f32[512,512]{1,0:T(8,128)}, f32[512,512]{1,0:T(8,128)}, f32[512,512]{1,0:T(8,128)}, /*inde...) custom-call(bf16[512,6144]{1,0:T(8,128)(2,1)S(1)} %copy-done, ...), custom_call_target="tpu_custom_call" | custom-call | tf_op jit(solution)/shard_map/widen/pallas_call | solution.py:1255
  213.2 0.5 slice_bitcast_fusion
Async XLA Ops:
  200.7 2.8 %copy-start = (bf16[512,6144]{1,0:T(8,128)(2,1)S(1)}, bf16[512,6144]{1,0:T(8,128)(2,1)}, u32[]{:S(2)}) copy-start(bf16[512,6144]{1,0:T(8,128)(2,1)} %get-tuple-element.30.ga.gb.gc) | copy-start | bytes 18874372
  203.5 1.2 copy-start.1
  204.7 1.2 copy-start.2
  205.9 0.7 copy-start.3
